TPU v7x, 32 devices: a whole 2x2x4 slice. The times are simulated.
32 devices in a mesh: ens: 2 (over x), lat: 4 (over y, core), lon: 4 (over z).
Axes of the slice: x: 2, y: 2, z: 4, core: 2. Of those that a mesh axis runs over, the one named last changes fastest.
Arguments:
- starting_state: bfloat16 [4, 222, 128, 512], P('ens', None, 'lat', 'lon'), may hold values from -6 to 6
- random_fields: bfloat16 [4, 16, 128, 512], P('ens', None, 'lat', 'lon'), may hold values from -6 to 6
- observed: float32 [6, 13, 128, 512], P(None, None, 'lat', 'lon'), may hold values from -6 to 6
- input_weight: bfloat16 [256, 222], replicated, may hold values from -0.375 to 0.375
- random_weight: bfloat16 [256, 16], replicated, may hold values from -1.5 to 1.5
- hidden_weight: bfloat16 [256, 256], replicated, may hold values from -0.375 to 0.375
- output_weight: bfloat16 [222, 256], replicated, may hold values from -0.375 to 0.375
- diffusivity: float32 [222], replicated, may hold values from 0.02 to 0.24
Outputs:
- grad_state: bfloat16 [4, 222, 128, 512], P('ens', None, 'lat', 'lon')
- grad_w_in: float32 [256, 222], replicated
- grad_w_noise: float32 [256, 16], replicated
- grad_w_mid: float32 [256, 256], replicated
- grad_w_out: float32 [222, 256], replicated
- grad_diffusivity: float32 [222], replicated
All inputs are finite; a program needn't handle non-finite values.
Results may differ from a plain program's by a relative error of at most 0.008.
Values may be sent and summed in bfloat16 or wider, within the bound.
No kernel may reach another device: no remote copies, remote signals or barrier semaphores. Data moves between devices by JAX's collectives and lax.ppermute only.
A program may use at most 128 MiB of HBM per device.

v0:
```python
import functools

import jax
import jax.numpy as jnp
import numpy as np
from jax import lax
from jax.experimental import pallas as pl
from jax.experimental.pallas import tpu as pltpu
from jax.sharding import PartitionSpec as P


PROGNOSTIC_COUNT = 6
LEVEL_COUNT = 37
SCORED = 13
DELTA = 0.1
SUB = 8

F32 = jnp.float32
BF16 = jnp.bfloat16


def round_up(value, step):
    return -(-value // step) * step


def channel_order():
    return [
        v * LEVEL_COUNT + level
        for first in range(3)
        for v in range(PROGNOSTIC_COUNT)
        for level in range(first, LEVEL_COUNT, 3)
    ]


def nt(a, b, **kw):
    return lax.dot_general(a, b, (((1,), (1,)), ((), ())), preferred_element_type=F32, **kw)


def tn(a, b, **kw):
    return lax.dot_general(a, b, (((0,), (0,)), ((), ())), preferred_element_type=F32, **kw)


def nn(a, b, **kw):
    return lax.dot_general(a, b, (((1,), (0,)), ((), ())), preferred_element_type=F32, **kw)


def softened_slope(diff):
    return diff * lax.rsqrt(diff * diff + DELTA * DELTA)


def params(**kw):
    return pltpu.CompilerParams(vmem_limit_bytes=10 << 20, **kw)


def put_edges(edge_ref, value, place, lanes):
    moved = pltpu.roll(value, place, axis=1)
    before = lax.rem(place + lanes - 1, lanes)
    lane = lax.broadcasted_iota(jnp.int32, value.shape, 1)
    edge_ref[...] = jnp.where((lane == place) | (lane == before), moved, edge_ref[...])


def transpose_kernel(order, channels, weights, st_ref, rf_ref, *refs):
    sources, (t_ref, lo_ref, hi_ref, edge_ref), prepared = refs[:weights], refs[weights : weights + 4], refs[weights + 4 : -2]
    nat, edge = refs[-2:]
    m, rb = pl.program_id(0), pl.program_id(1)
    state_rows = edge_ref.shape[0]
    noise = rf_ref.shape[1]
    lanes = st_ref.shape[3]
    span = 2 * SUB * pl.num_programs(1)

    @pl.when((m == 0) & (rb == 0))
    def _():
        edge[...] = jnp.zeros_like(edge)
        nat[channels * SUB : state_rows * SUB, :] = jnp.zeros(
            ((state_rows - channels) * SUB, lanes), F32
        )

    for place, c in enumerate(order):
        nat[place * SUB : (place + 1) * SUB, :] = st_ref[0, c].astype(F32)
    for k in range(noise):
        place = state_rows + k
        nat[place * SUB : (place + 1) * SUB, :] = rf_ref[0, k].astype(F32)
    for s in range(SUB):
        row = nat[pl.ds(s, state_rows + noise, stride=SUB), :]
        t_ref[m, rb * SUB + s] = row
        put_edges(edge, row[:state_rows], m * span + 2 * (rb * SUB + s), lanes)

    edge_ref[...] = edge[...].astype(BF16)

    @pl.when((m == pl.num_programs(0) - 1) & (rb == pl.num_programs(1) - 1))
    def _():
        choose_rows(
            t_ref[:, 0, :state_rows], t_ref[:, t_ref.shape[1] - 1, :state_rows], lo_ref, hi_ref
        )
        prepare(*sources, *prepared)


def choose_rows(low, high, first_ref, second_ref):
    even = lax.axis_index("lat") % 2 == 0
    first_ref[...] = jnp.where(even, high, low).astype(BF16)
    second_ref[...] = jnp.where(even, low, high).astype(BF16)


def prepare(
    win_ref, wnoise_ref, wmid_ref, wout_ref, diff_ref, place_ref, placed_ref, scat_ref, shift_ref,
    in_ref, in_half_ref, mid_half_ref, out_ref, out_half_ref, coef_ref,
):
    w_in = tn(win_ref[...], placed_ref[...])
    w_in = w_in + tn(wnoise_ref[...], shift_ref[...])
    in_ref[...] = w_in.astype(BF16)
    in_half_ref[...] = (w_in * 0.5).astype(BF16)
    mid_half_ref[...] = (wmid_ref[...].astype(F32) * 0.5).astype(BF16)
    w_out = tn(scat_ref[...], wout_ref[...])
    out_ref[...] = w_out.astype(BF16)
    out_half_ref[...] = (w_out * 0.5).astype(BF16)
    state_rows, lanes = coef_ref.shape
    spread = jnp.broadcast_to(diff_ref[...], (lanes, diff_ref.shape[1]))
    coef_ref[...] = nt(
        place_ref[:state_rows].astype(F32), spread, precision=lax.Precision.HIGHEST
    )


def observed_kernel(scored, obs_ref, out_ref, nat):
    lat_rows, rows = out_ref.shape[:2]
    nat[scored * SUB :, :] = jnp.zeros(((rows - scored) * SUB, nat.shape[1]), F32)

    def block(rb, _):
        first = pl.multiple_of(rb * SUB, SUB)
        for c in range(scored):
            nat[c * SUB : (c + 1) * SUB, :] = obs_ref[c, pl.ds(first, SUB), :]
        for s in range(SUB):
            out_ref[first + s] = nat[pl.ds(s, rows, stride=SUB), :]
        return 0

    lax.fori_loop(0, lat_rows // SUB, block, 0)


def stencil_setup(left_ref, right_ref, halo, weights):
    lanes = halo.shape[1]
    lane = lax.broadcasted_iota(jnp.int32, halo.shape, 1)
    from_left = pltpu.roll(left_ref[...].astype(F32), 1, axis=1)
    from_right = pltpu.roll(right_ref[...].astype(F32), lanes - 1, axis=1)
    halo[...] = jnp.where(lane % 2 == 0, from_left, from_right)
    k = lax.broadcasted_iota(jnp.int32, (lanes, lanes), 0)
    lane = lax.broadcasted_iota(jnp.int32, (lanes, lanes), 1)
    beside = jnp.where((k == lane + 1) | (k + 1 == lane), 1.0, 0.0) - jnp.where(k == lane, 4.0, 0.0)
    ends = jnp.where((k == lane) & ((k == 0) | (k == lanes - 1)), 1.0, 0.0)
    weights[:lanes, :] = beside.astype(BF16)
    weights[lanes:, :] = ends.astype(BF16)


def stencil_rows(load, halo, weights, base, rows, store):
    lanes = halo.shape[1]
    for i in range(rows):
        turned = pltpu.roll(halo[...], lax.rem(2 * lanes - base - 2 * i, lanes), axis=1)
        row = load(i)
        ends = jnp.concatenate([row.astype(BF16), turned.astype(BF16)], axis=1)
        store(i, row, nn(ends, weights[...]) + load(i - 1) + load(i + 1))


def activate(half):
    gate = jnp.tanh(half)
    part = half * gate
    return half + part, (1.0 + gate) * (1.0 + (half - part))


def forward_kernel(
    first_row, rows, scored, member_span, t_ref, up_ref, dn_ref, left_ref, right_ref, coef_ref, win_ref, wmid_ref,
    wout_ref, f_ref, x_ref, lap_ref, act1_ref, slope1_ref, act2_ref, slope2_ref, keep, around, weights,
):
    state_rows, lanes = coef_ref.shape
    kept = keep.shape[0]
    stencil_setup(left_ref, right_ref, around, weights)
    even = lax.axis_index("lat") % 2 == 0

    def member(m, _):
        def load(i):
            if i < 0 and up_ref is not None:
                return jnp.where(even, up_ref[1][m].astype(F32), up_ref[0][m].astype(F32))
            if i == rows and dn_ref is not None:
                return jnp.where(even, dn_ref[0][m].astype(F32), dn_ref[1][m].astype(F32))
            return t_ref[m, first_row + i, :state_rows, :]

        def store(i, row, lap):
            stepped = row + coef_ref[...] * lap
            at = i * lanes
            x_ref[m, :state_rows, at : at + lanes] = stepped.astype(BF16)
            lap_ref[m, i] = lap.astype(BF16)
            keep[:, at : at + lanes] = stepped[:kept]

        stencil_rows(load, around, weights, m * member_span + 2 * first_row, rows, store)
        for i in range(rows):
            x_ref[m, state_rows:, i * lanes : (i + 1) * lanes] = t_ref[
                m, first_row + i, state_rows:, :
            ].astype(BF16)
        width = min(4, rows) * lanes
        scored_row = lax.broadcasted_iota(jnp.int32, (kept, lanes), 0) < scored
        for at in range(0, rows * lanes, width):
            cols = slice(at, at + width)
            act1, slope1 = activate(nn(win_ref[...], x_ref[m, :, cols]))
            act1_ref[m, :, cols] = act1.astype(BF16)
            slope1_ref[m, :, cols] = slope1.astype(BF16)
            act2, slope2 = activate(nn(wmid_ref[...], act1.astype(BF16)))
            act2_ref[m, :, cols] = act2.astype(BF16)
            slope2_ref[m, :, cols] = slope2.astype(BF16)
            out = nn(wout_ref[...], act2.astype(BF16)) + keep[:, cols]
            for j in range(width // lanes):
                piece = out[:, j * lanes : (j + 1) * lanes]
                f_ref[m, at // lanes + j] = jnp.where(scored_row, piece, 0.0).astype(BF16)
        return 0

    lax.fori_loop(0, t_ref.shape[0], member, 0)


def backward_kernel(
    partners, first, last, first_row, spread, own_ref, *refs
):
    other_refs = refs[:partners]
    (
        obs_ref, x_ref, lap_ref, act1_ref, slope1_ref, act2_ref, slope2_ref, win_ref, wmid_ref, wout_ref,
    ) = refs[partners : partners + 10]
    refs = refs[partners + 10 :]
    in_refs = ()
    if not first:
        in_refs, refs = refs[:6], refs[6:]
    grad_ref, *acc_refs = refs[:6]
    refs = refs[6:]
    if last:
        first_ref, second_ref, refs = refs[0], refs[1], refs[2:]
    score, edge = refs[-2:]
    part_refs = refs[:-2]
    members, chunk_rows, kept, lanes = own_ref.shape
    rows = score.shape[2] // lanes
    total_members = members * (partners + 1)
    state_rows = lap_ref.shape[2]
    in_acc, mid_acc, out_acc, diff_acc, edge_out = acc_refs

    if first:
        for ref in (in_acc, mid_acc, out_acc, diff_acc):
            ref[...] = jnp.zeros_like(ref)
        edge[...] = jnp.zeros_like(edge)
    else:
        for ref, old in zip((in_acc, mid_acc, out_acc, diff_acc), in_refs[:4], strict=True):
            ref[...] = old[...]
        edge[...] = in_refs[4][...].astype(F32)

    def part(step, _):
        for i in range(rows):
            row = step * rows + i
            target = obs_ref[first_row + row]
            own = [own_ref[m, row].astype(F32) for m in range(members)]
            pairs = [jnp.zeros_like(target) for _ in range(members)]
            for m in range(members):
                for k in range(m + 1, members):
                    slope = softened_slope(own[m] - own[k])
                    pairs[m] = pairs[m] + slope
                    pairs[k] = pairs[k] - slope
                for other in other_refs:
                    for k in range(members):
                        pairs[m] = pairs[m] + softened_slope(own[m] - other[k, row].astype(F32))
            for m in range(members):
                grad = softened_slope(own[m] - target) - pairs[m] * (1.0 / (total_members - 1.0))
                score[m, :, i * lanes : (i + 1) * lanes] = grad.astype(BF16)
        diff = diff_acc[...]
        cols = pl.ds(pl.multiple_of(step * (rows * lanes), lanes), rows * lanes)
        for m in range(members):
            grad = score[m]
            out_acc[...] += nt(grad, act2_ref[m, :, cols])
            delta2 = (tn(wout_ref[...], grad) * slope2_ref[m, :, cols].astype(F32)).astype(BF16)
            mid_acc[...] += nt(delta2, act1_ref[m, :, cols])
            delta1 = (tn(wmid_ref[...], delta2) * slope1_ref[m, :, cols].astype(F32)).astype(BF16)
            in_acc[...] += nt(x_ref[m, :, cols], delta1)
            stepped_grad = tn(win_ref[...], delta1)[:state_rows]
            for i in range(rows):
                row = step * rows + i
                piece = stepped_grad[:, i * lanes : (i + 1) * lanes]
                top = piece[:kept] + grad[:, i * lanes : (i + 1) * lanes].astype(F32)
                piece = jnp.concatenate([top, piece[kept:]], axis=0)
                diff = diff + piece * lap_ref[m, row].astype(F32)
                grad_ref[m, first_row + row] = piece
                put_edges(edge, piece, m * spread + 2 * (first_row + row), lanes)
        diff_acc[...] = diff
        return 0

    lax.fori_loop(0, chunk_rows // rows, part, 0)
    edge_out[...] = edge[...].astype(BF16)
    if last:
        low = grad_ref[:, 0] if first else in_refs[5][:, 0]
        choose_rows(low, grad_ref[:, first_row + chunk_rows - 1], first_ref, second_ref)
        pack_ref, part_refs = part_refs[-1], part_refs[:-1]
        at = 0
        for acc in (in_acc, mid_acc, out_acc):
            pack_ref[at : at + acc.shape[0], :] = acc[...].astype(BF16)
            at += acc.shape[0]
        sums = nt(jnp.ones((8, lanes), F32), diff_acc[...], precision=lax.Precision.HIGHEST)
        pack_ref[at:, :] = jnp.zeros((pack_ref.shape[0] - at, pack_ref.shape[1]), BF16)
        pack_ref[at : at + 8, :state_rows] = sums.astype(BF16)
        split_halves(1, pack_ref, *part_refs)


def halves(bit, height):
    mine = lax.axis_index("lat") // bit % 2
    return (pl.ds(pl.multiple_of(side * height, 8), height) for side in (mine, 1 - mine))


def split_halves(bit, value_ref, mine_ref, other_ref):
    mine, other = halves(bit, mine_ref.shape[0])
    mine_ref[...] = value_ref[mine, :]
    other_ref[...] = value_ref[other, :]


def join_halves(bit, mine_ref, other_ref, value_ref):
    mine, other = halves(bit, mine_ref.shape[0])
    value_ref[mine, :] = mine_ref[...]
    value_ref[other, :] = other_ref[...]


def sum_kernel(bit, inputs, *refs):
    total = refs[0][...].astype(F32)
    for ref in refs[1:inputs]:
        total = total + ref[...].astype(F32)
    if bit is None:
        refs[inputs][...] = total.astype(BF16)
    else:
        refs[-1][...] = total.astype(BF16)
        split_halves(bit, refs[-1], *refs[inputs:-1])


def final_kernel(
    order, member_span, rows, first, stride, chunks, g_ref, first_ref, second_ref, left_ref, right_ref, coef_ref, *refs
):
    out_ref, nat, around, weights = refs[-4:]
    m, index = pl.program_id(0), first + pl.program_id(1) * stride
    first_row = index * rows
    state_rows = g_ref.shape[2]
    even = lax.axis_index("lat") % 2 == 0

    @pl.when((m == 0) & (pl.program_id(1) == 0))
    def _():
        stencil_setup(left_ref, right_ref, around, weights)

    def load(i):
        if i < 0:
            halo = jnp.where(even, second_ref[m].astype(F32), first_ref[m].astype(F32))
            return jnp.where(index == 0, halo, g_ref[m, jnp.maximum(first_row - 1, 0)])
        if i == rows:
            inner = g_ref[m, jnp.minimum(first_row + rows, g_ref.shape[1] - 1)]
            halo = jnp.where(even, first_ref[m].astype(F32), second_ref[m].astype(F32))
            return jnp.where(index == chunks - 1, halo, inner)
        return g_ref[m, first_row + i]

    def store(i, row, lap):
        nat[pl.ds(i, state_rows, stride=SUB), :] = row + coef_ref[...] * lap

    stencil_rows(load, around, weights, m * member_span + 2 * first_row, rows, store)
    for place, c in enumerate(order):
        out_ref[0, c] = nat[place * SUB : (place + 1) * SUB, :].astype(BF16)


def unpack_kernel(
    channels, noise, inverse_count, mine_ref, other_ref, place_ref, scat_ref, win_ref, wnoise_ref, mid_ref, out_ref,
    diff_ref, pack_ref,
):
    join_halves(1, mine_ref, other_ref, pack_ref)
    hidden = mid_ref.shape[0]
    total, kept = place_ref.shape[0], scat_ref.shape[1]
    state_rows = total - noise
    win_ref[...] = tn(place_ref[:, :channels], pack_ref[:total, :]) * inverse_count
    wnoise_ref[...] = pack_ref[state_rows:total, :].astype(F32) * inverse_count
    at = total
    mid_ref[...] = pack_ref[at : at + hidden, :].astype(F32) * inverse_count
    at += hidden
    out_ref[...] = nn(scat_ref[...], pack_ref[at : at + kept, :]) * inverse_count
    at += kept
    diff = nn(pack_ref[at : at + 8, :state_rows], place_ref[:state_rows, :channels])
    diff_ref[...] = diff[0:1] * inverse_count


def in_hbm(value):
    return pltpu.with_memory_space_constraint(value, pltpu.HBM)


def in_vmem(value):
    return pltpu.with_memory_space_constraint(value, pltpu.VMEM)


RESIDENT = pl.BlockSpec(memory_space=pltpu.VMEM)


def ring(axis, shift):
    count = lax.axis_size(axis)
    return [(i, (i + shift) % count) for i in range(count)]


def swap(value, start):
    pairs = [(i, i + 1) for i in range(start, lax.axis_size("lat") - 1, 2)]
    return lax.ppermute(value, "lat", [*pairs, *((b, a) for a, b in pairs)])


def across(value, bit):
    return lax.ppermute(value, "lat", [(i, i ^ bit) for i in range(lax.axis_size("lat"))])


def everyone(value, axis):
    return [value, *[lax.ppermute(value, axis, ring(axis, k)) for k in range(1, lax.axis_size(axis))]]


def add_parts(parts, bit=None):
    height, width = parts[0].shape
    count = 1 if bit is None else 2
    return pl.pallas_call(
        functools.partial(sum_kernel, bit, len(parts)),
        in_specs=[RESIDENT] * len(parts),
        out_specs=[RESIDENT] * count,
        out_shape=[pltpu.VMEM((height // count, width), BF16)] * count,
        scratch_shapes=[] if bit is None else [pltpu.VMEM((height, width), BF16)],
        compiler_params=params(),
        name="add_parts",
    )(*map(in_vmem, parts))


def join(bit, mine, other):
    height, width = mine.shape
    return pl.pallas_call(
        functools.partial(join_halves, bit),
        in_specs=[RESIDENT] * 2,
        out_specs=RESIDENT,
        out_shape=pltpu.VMEM((height * 2, width), BF16),
        compiler_params=params(),
        name="join_halves",
    )(in_vmem(mine), in_vmem(other))


def on_device(
    starting_state, random_fields, observed, input_weight, random_weight, hidden_weight, output_weight, diffusivity
):
    members, channels, lat_rows, lanes = starting_state.shape
    noise = random_fields.shape[1]
    hidden = hidden_weight.shape[0]
    scored = PROGNOSTIC_COUNT * SCORED
    kept = round_up(scored, 16)
    state_rows = round_up(channels, 32)
    total = state_rows + noise
    span = 2 * lat_rows
    order = channel_order()
    blocks = lat_rows // SUB
    chunk = SUB
    chunks = lat_rows // chunk
    cells = chunk * lanes
    partners = lax.axis_size("ens") - 1
    assert members * span <= lanes and lat_rows % SUB == 0
    lat_n, lon_n = lax.axis_size("lat"), lax.axis_size("lon")
    assert lat_n > 1 and lat_n & (lat_n - 1) == 0

    place = np.zeros((total, channels), np.float32)
    for at, c in enumerate(order):
        place[at, c] = 1.0
    scatter = np.zeros((channels, kept), np.float32)
    for at, c in enumerate(order[:scored]):
        scatter[c, at] = 1.0
    shift = np.zeros((noise, total), np.float32)
    for k in range(noise):
        shift[k, state_rows + k] = 1.0
    place, placed, scatter, shift = (jnp.asarray(x, BF16) for x in (place, place.T, scatter, shift))
    sources = [
        input_weight.T, random_weight.T, hidden_weight, output_weight, diffusivity.reshape(1, channels),
        place, placed, scatter, shift,
    ]

    whole2 = lambda shape: pl.BlockSpec(shape, lambda *_: (0,) * len(shape))

    rows_t, low, high, edge, w_in, w_in_half, w_mid_half, w_out, w_out_half, coef = pl.pallas_call(
        functools.partial(transpose_kernel, order, channels, len(sources)),
        grid=(members, blocks),
        in_specs=[
            pl.BlockSpec((1, channels, SUB, lanes), lambda m, r: (m, 0, r, 0)),
            pl.BlockSpec((1, noise, SUB, lanes), lambda m, r: (m, 0, r, 0)),
            *[whole2(x.shape) for x in sources],
        ],
        out_specs=[RESIDENT] * 10,
        out_shape=[
            pltpu.VMEM((members, lat_rows, total, lanes), F32),
            pltpu.VMEM((members, state_rows, lanes), BF16),
            pltpu.VMEM((members, state_rows, lanes), BF16),
            pltpu.VMEM((state_rows, lanes), BF16),
            pltpu.VMEM((hidden, total), BF16),
            pltpu.VMEM((hidden, total), BF16),
            pltpu.VMEM((hidden, hidden), BF16),
            pltpu.VMEM((kept, hidden), BF16),
            pltpu.VMEM((kept, hidden), BF16),
            pltpu.VMEM((state_rows, lanes), F32),
        ],
        scratch_shapes=[
            pltpu.VMEM((total * SUB, lanes), F32),
            pltpu.VMEM((state_rows, lanes), F32),
        ],
        compiler_params=params(),
        name="transpose",
    )(in_hbm(starting_state), in_hbm(random_fields), *map(in_hbm, sources))
    sides = [lax.ppermute(edge, "lon", ring("lon", k)) for k in (1, -1)]

    target = pl.pallas_call(
        functools.partial(observed_kernel, scored),
        in_specs=[RESIDENT],
        out_specs=RESIDENT,
        out_shape=pltpu.VMEM((lat_rows, kept, lanes), F32),
        scratch_shapes=[pltpu.VMEM((kept * SUB, lanes), F32)],
        compiler_params=params(),
        name="observed",
    )(in_vmem(observed.reshape(scored, lat_rows, lanes)))

    def forward(index, swapped):
        first_row = index * chunk
        at_start, at_end = index == 0, index == chunks - 1
        halo = list(swapped) if at_start or at_end else []

        def body(t_ref, *refs):
            got, refs = refs[: len(halo)], refs[len(halo) :]
            up, down = got if at_start else None, got if at_end else None
            forward_kernel(first_row, chunk, scored, span, t_ref, up, down, *refs)

        return pl.pallas_call(
            body,
            in_specs=[RESIDENT] * (7 + len(halo)),
            out_specs=[RESIDENT] * 7,
            out_shape=[
                pltpu.VMEM((members, chunk, kept, lanes), BF16),
                pltpu.VMEM((members, total, cells), BF16),
                pltpu.VMEM((members, chunk, state_rows, lanes), BF16),
                *[pltpu.VMEM((members, hidden, cells), BF16) for _ in range(4)],
            ],
            scratch_shapes=[
                pltpu.VMEM((kept, cells), F32),
                pltpu.VMEM((state_rows, lanes), F32),
                pltpu.VMEM((2 * lanes, lanes), BF16),
            ],
            compiler_params=params(),
        )(in_vmem(rows_t), *halo, *sides, coef, w_in_half, w_mid_half, w_out)

    pack_rows = round_up(total + hidden + kept + 8, 16 * lat_n)

    def backward(index, residuals, others, carried, grads):
        own, x, lap, act1, slope1, act2, slope2 = residuals
        first, last = index == chunk_order[0], index == chunk_order[-1]
        rows = 4
        accs = [(total, hidden), (hidden, hidden), (kept, hidden), (state_rows, lanes), (state_rows, lanes)]
        acc_types = [F32, F32, F32, F32, BF16]
        inputs = [
            *map(in_vmem, (own, *others, target, x, lap, act1, slope1, act2, slope2)),
            w_in, w_mid_half, w_out_half, *map(in_vmem, carried), *([] if first else [in_vmem(grads)]),
        ]
        outputs = [
            pltpu.VMEM((members, lat_rows, state_rows, lanes), F32),
            *[pltpu.VMEM(shape, kind) for shape, kind in zip(accs, acc_types, strict=True)],
            *([pltpu.VMEM((members, state_rows, lanes), BF16)] * 2 if last else []),
            *([pltpu.VMEM((pack_rows // 2, hidden), BF16)] * 2 if last else []),
        ]
        return pl.pallas_call(
            functools.partial(backward_kernel, partners, first, last, index * chunk, span),
            in_specs=[RESIDENT] * len(inputs),
            out_specs=[RESIDENT] * len(outputs),
            out_shape=outputs,
            input_output_aliases={} if first else {len(inputs) - 1: 0},
            scratch_shapes=[
                *([pltpu.VMEM((pack_rows, hidden), BF16)] if last else []),
                pltpu.VMEM((members, kept, rows * lanes), BF16),
                pltpu.VMEM((state_rows, lanes), F32),
            ],
            compiler_params=params(),
        )(*inputs)

    chunk_order = [*range(1, chunks - 1), 0, chunks - 1] if chunks > 1 else [0]
    saved, received = {}, {}
    swapped = None
    for index in chunk_order:
        if index == 0:
            swapped = swap(low, 0), swap(high, 1)
        saved[index] = forward(index, swapped)
        received[index] = [
            lax.ppermute(saved[index][0], "ens", ring("ens", k)) for k in range(1, partners + 1)
        ]
    grads, carried = None, []
    for index in chunk_order:
        grads, *carried = backward(index, saved[index], received[index], carried, grads)
        carried, more = carried[:5], carried[5:]
    edge, (low, high, mine, other) = carried[-1], more
    first = swap(low, 0)
    swapped = first, swap(high, 1)
    left = lax.ppermute(edge, "lon", ring("lon", 1))
    sides = left, lax.ppermute(edge, "lon", ring("lon", -1))

    def final(which, out):
        inputs = [*map(in_vmem, (grads, *swapped, *sides)), coef]
        first, stride = which[0], which[-1] - which[0]
        index_map = lambda m, j: (m, 0, first + j * stride, 0)
        return pl.pallas_call(
            functools.partial(final_kernel, order, span, chunk, first, stride, chunks),
            grid=(members, len(which)),
            in_specs=[
                *[RESIDENT] * len(inputs),
                *([] if out is None else [pl.BlockSpec(memory_space=pl.ANY)]),
            ],
            out_specs=pl.BlockSpec((1, channels, chunk, lanes), index_map),
            out_shape=pltpu.HBM(starting_state.shape, BF16),
            scratch_shapes=[
                pltpu.VMEM((state_rows * SUB, lanes), F32),
                pltpu.VMEM((state_rows, lanes), F32),
                pltpu.VMEM((2 * lanes, lanes), BF16),
            ],
            input_output_aliases={} if out is None else {len(inputs): 0},
            compiler_params=params(),
            name="final",
        )(*inputs, *([] if out is None else [out]))

    bits = [1 << k for k in range(lat_n.bit_length() - 1)]
    for bit in bits:
        parts = [mine, across(other, bit)]
        parts = add_parts(parts, None if bit == bits[-1] else 2 * bit)
        mine, other = parts[0], parts[-1]
    parts = everyone(mine, "ens")
    (mine,) = add_parts(parts)
    parts = everyone(mine, "lon")
    grad_state = final(chunk_order[:-2], None)
    (mine,) = add_parts(parts)
    for bit in bits[::-1]:
        other = across(mine, bit)
        if bit != bits[0]:
            mine = join(bit, mine, other)
    parts = [mine, other]
    grad_state = final(chunk_order[-2:], grad_state)
    count = members * (partners + 1) * lat_rows * lat_n * lanes * lon_n
    g_in, g_noise, g_mid, g_out, g_diff = pl.pallas_call(
        functools.partial(unpack_kernel, channels, noise, 1.0 / count),
        out_shape=[
            jax.ShapeDtypeStruct((channels, hidden), F32),
            jax.ShapeDtypeStruct((noise, hidden), F32),
            jax.ShapeDtypeStruct((hidden, hidden), F32),
            jax.ShapeDtypeStruct((channels, hidden), F32),
            jax.ShapeDtypeStruct((1, channels), F32),
        ],
        scratch_shapes=[pltpu.VMEM((pack_rows, hidden), BF16)],
        compiler_params=params(),
        name="unpack",
    )(*map(in_vmem, parts), place, scatter)
    return grad_state, g_in.T, g_noise.T, g_mid, g_out, g_diff.reshape(channels)


def solution(mesh):
    tiles = P("ens", None, "lat", "lon")
    in_specs = (tiles, tiles, P(None, None, "lat", "lon"), P(), P(), P(), P(), P())
    out_specs = (tiles, P(), P(), P(), P(), P())

    return jax.shard_map(on_device, mesh=mesh, in_specs=in_specs, out_specs=out_specs, check_vma=False)
```

profile of v0, /device:TPU:0, one launch (start us, length us, event | category | flops | bytes accessed | tf_op | source)
XLA Modules:
  0.0 95.4 jit_solution(2179618836298627183)
XLA Ops:
  0.6 7.2 %transpose.17 = (f32[2,32,240,128]{3,2,1,0:T(8,128)S(1)}, bf16[2,224,128]{2,1,0:T(8,128)(2,1)S(1)}, bf16[2,224,128]{2,1,0:T(8,128)(2,1)S(1)}, bf16[224,128]{1,0:...) custom-call(bf16[2,222,32,128]{3,2,1,0:T(8,128)(2,1)} %st_ref.1, ...), custom_call_target="tpu_custom_call" | custom-call | tf_op jit(solution)/shard_map/transpose/pallas_call | solution.py:472
  7.8 0.6 collective-permute-start
  8.4 0.7 collective-permute-start.1
  9.0 2.6 %collective-permute-start.2 = (bf16[224,128]{1,0:T(8,128)(2,1)S(1)}, bf16[224,128]{1,0:T(8,128)(2,1)S(1)}, u32[]{:S(2)}, u32[]{:S(2)}) collective-permute-start(bf16[224,128]{1,0:T(8,128)(2,1)S(1)} %get-tuple-element.78), channel_id=1, source_target_pairs={{0,1},{1,2},{2,3},{3,0},{4,5},{5,6},{6,7},{7,4},{8,9},{9,10},{10,1... | collective-permute-start | bytes 172040 | tf_op jit(solution)/shard_map/ppermute | solution.py:500
  11.7 2.1 %collective-permute-start.3 = (bf16[224,128]{1,0:T(8,128)(2,1)S(1)}, bf16[224,128]{1,0:T(8,128)(2,1)S(1)}, u32[]{:S(2)}, u32[]{:S(2)}) collective-permute-start(bf16[224,128]{1,0:T(8,128)(2,1)S(1)} %get-tuple-element.78), channel_id=1, source_target_pairs={{0,3},{1,0},{2,1},{3,2},{4,7},{5,4},{6,5},{7,6},{8,11},{9,8},{10,9... | collective-permute-start | bytes 172040 | tf_op jit(solution)/shard_map/ppermute | solution.py:500
  13.8 2.2 %collective-permute-done.2.refs_2_.refs_0_ = bf16[224,128]{1,0:T(8,128)(2,1)S(1)} collective-permute-done((bf16[224,128]{1,0:T(8,128)(2,1)S(1)}, bf16[224,128]{1,0:T(8,128)(2,1)S(1)}, u32[]{:S(2)}, u32[]{:S(2)}) %collective-permute-start.2) | collective-permute-done | bytes 57376 | tf_op jit(solution)/shard_map/ppermute | solution.py:500
  16.0 0.5 collective-permute-done.3.refs_3_.refs_1_
  16.5 3.6 %shard_map.166 = (bf16[2,8,80,128]{3,2,1,0:T(8,128)(2,1)S(1)}, bf16[2,240,1024]{2,1,0:T(8,128)(2,1)S(1)}, bf16[2,8,224,128]{3,2,1,0:T(8,128)(2,1)S(1)}, bf16[2,2...) custom-call(f32[2,32,240,128]{3,2,1,0:T(8,128)S(1)} %get-tuple-eleme, ...), custom_call_target="tpu_custom_call" | custom-call | tf_op jit(solution)/shard_map/pallas_call | solution.py:522
  20.1 1.6 %collective-permute-start.7 = (bf16[2,8,80,128]{3,2,1,0:T(8,128)(2,1)S(1)}, bf16[2,8,80,128]{3,2,1,0:T(8,128)(2,1)S(1)}, u32[]{:S(2)}, u32[]{:S(2)}) collective-permute-start(bf16[2,8,80,128]{3,2,1,0:T(8,128)(2,1)S(1)} %get-tuple-element.106.own_ref), channel_id=1, source_target_pairs={{0,16},{16,0},{1,17},{17,1},{2,18},{18,2},{3,19},{19,3},{4,20},{20... | collective-permute-start | bytes 983048 | tf_op jit(solution)/shard_map/ppermute | solution.py:580
  21.6 3.6 %shard_map.165 = (bf16[2,8,80,128]{3,2,1,0:T(8,128)(2,1)S(1)}, bf16[2,240,1024]{2,1,0:T(8,128)(2,1)S(1)}, bf16[2,8,224,128]{3,2,1,0:T(8,128)(2,1)S(1)}, bf16[2,2...) custom-call(f32[2,32,240,128]{3,2,1,0:T(8,128)S(1)} %get-tuple-eleme, ...), custom_call_target="tpu_custom_call" | custom-call | tf_op jit(solution)/shard_map/pallas_call | solution.py:522
  25.2 0.0 copy-start
  25.2 0.6 collective-permute-start.6
  25.8 0.0 collective-permute-done.refs_0_
  25.8 3.6 %shard_map.164 = (bf16[2,8,80,128]{3,2,1,0:T(8,128)(2,1)S(1)}, bf16[2,240,1024]{2,1,0:T(8,128)(2,1)S(1)}, bf16[2,8,224,128]{3,2,1,0:T(8,128)(2,1)S(1)}, bf16[2,2...) custom-call(f32[2,32,240,128]{3,2,1,0:T(8,128)S(1)} %get-tuple-eleme, ...), custom_call_target="tpu_custom_call" | custom-call | tf_op jit(solution)/shard_map/pallas_call | solution.py:522
  29.4 1.6 %collective-permute-start.5 = (bf16[2,8,80,128]{3,2,1,0:T(8,128)(2,1)S(1)}, bf16[2,8,80,128]{3,2,1,0:T(8,128)(2,1)S(1)}, u32[]{:S(2)}, u32[]{:S(2)}) collective-permute-start(bf16[2,8,80,128]{3,2,1,0:T(8,128)(2,1)S(1)} %get-tuple-element.92.own_ref), channel_id=1, source_target_pairs={{0,16},{16,0},{1,17},{17,1},{2,18},{18,2},{3,19},{19,3},{4,20},{20... | collective-permute-start | bytes 983048 | tf_op jit(solution)/shard_map/ppermute | solution.py:580
  31.0 3.6 %shard_map.163 = (bf16[2,8,80,128]{3,2,1,0:T(8,128)(2,1)S(1)}, bf16[2,240,1024]{2,1,0:T(8,128)(2,1)S(1)}, bf16[2,8,224,128]{3,2,1,0:T(8,128)(2,1)S(1)}, bf16[2,2...) custom-call(f32[2,32,240,128]{3,2,1,0:T(8,128)S(1)} %get-tuple-eleme, ...), custom_call_target="tpu_custom_call" | custom-call | tf_op jit(solution)/shard_map/pallas_call | solution.py:522
  34.6 0.6 collective-permute-start.4
  35.2 0.4 observed.1.refs_1_
  35.6 3.0 %shard_map.167 = (f32[2,32,224,128]{3,2,1,0:T(8,128)S(1)}, f32[240,256]{1,0:T(8,128)S(1)}, f32[256,256]{1,0:T(8,128)S(1)}, f32[80,256]{1,0:T(8,128)S(1)}, f32[22...) custom-call(bf16[2,8,80,128]{3,2,1,0:T(8,128)(2,1)S(1)} %get-tuple-element.106.own_ref, ...), custom_call_target="tpu_custom_call" | custom-call | tf_op jit(solution)/shard_map/pallas_call | solution.py:558
  38.6 3.0 %shard_map.168 = (f32[2,32,224,128]{3,2,1,0:T(8,128)S(1)}, f32[240,256]{1,0:T(8,128)S(1)}, f32[256,256]{1,0:T(8,128)S(1)}, f32[80,256]{1,0:T(8,128)S(1)}, f32[22...) custom-call(bf16[2,8,80,128]{3,2,1,0:T(8,128)(2,1)S(1)} %get-tuple-element.99.own_ref, ...), custom_call_target="tpu_custom_call", output_to_operand_aliasing={{0}: (17, {})} | custom-call | tf_op jit(solution)/shard_map/pallas_call | solution.py:558
  41.7 2.1 %collective-permute-done.5.refs_0_ = bf16[2,8,80,128]{3,2,1,0:T(8,128)(2,1)S(1)} collective-permute-done((bf16[2,8,80,128]{3,2,1,0:T(8,128)(2,1)S(1)}, bf16[2,8,80,128]{3,2,1,0:T(8,128)(2,1)S(1)}, u32[]{:S(2)}, u32[]{:S(2)}) %collective-permute-start.5) | collective-permute-done | bytes 327712 | tf_op jit(solution)/shard_map/ppermute | solution.py:580
  43.8 3.0 %shard_map.169 = (f32[2,32,224,128]{3,2,1,0:T(8,128)S(1)}, f32[240,256]{1,0:T(8,128)S(1)}, f32[256,256]{1,0:T(8,128)S(1)}, f32[80,256]{1,0:T(8,128)S(1)}, f32[22...) custom-call(bf16[2,8,80,128]{3,2,1,0:T(8,128)(2,1)S(1)} %get-tuple-element.92.own_ref, ...), custom_call_target="tpu_custom_call", output_to_operand_aliasing={{0}: (17, {})} | custom-call | tf_op jit(solution)/shard_map/pallas_call | solution.py:558
  46.8 4.0 %collective-permute-done.4.refs_0_ = bf16[2,8,80,128]{3,2,1,0:T(8,128)(2,1)S(1)} collective-permute-done((bf16[2,8,80,128]{3,2,1,0:T(8,128)(2,1)S(1)}, bf16[2,8,80,128]{3,2,1,0:T(8,128)(2,1)S(1)}, u32[]{:S(2)}, u32[]{:S(2)}) %collective-permute-start.4) | collective-permute-done | bytes 327712 | tf_op jit(solution)/shard_map/ppermute | solution.py:580
  50.8 4.0 %shard_map.170 = (f32[2,32,224,128]{3,2,1,0:T(8,128)S(1)}, f32[240,256]{1,0:T(8,128)}, f32[256,256]{1,0:T(8,128)}, f32[80,256]{1,0:T(8,128)}, f32[224,128]{1,0:T...) custom-call(bf16[2,8,80,128]{3,2,1,0:T(8,128)(2,1)S(1)} %get-tuple-e, ...), custom_call_target="tpu_custom_call", output_to_operand_aliasing={{0}: (17, {})} | custom-call | tf_op jit(solution)/shard_map/pallas_call | solution.py:558
  54.8 0.8 collective-permute-start.12
  55.6 1.0 %collective-permute-done.12.refs_1_ = bf16[320,256]{1,0:T(8,128)(2,1)S(1)} collective-permute-done((bf16[320,256]{1,0:T(8,128)(2,1)S(1)}, bf16[320,256]{1,0:T(8,128)(2,1)S(1)}, u32[]{:S(2)}, u32[]{:S(2)}) %collective-permute-start.12) | collective-permute-done | bytes 163872 | tf_op jit(solution)/shard_map/ppermute | solution.py:401
  56.6 0.1 add_parts.4
  56.7 0.4 collective-permute-start.13
  57.2 4.3 %collective-permute-done.13.refs_1_ = bf16[160,256]{1,0:T(8,128)(2,1)S(1)} collective-permute-done((bf16[160,256]{1,0:T(8,128)(2,1)S(1)}, bf16[160,256]{1,0:T(8,128)(2,1)S(1)}, u32[]{:S(2)}, u32[]{:S(2)}) %collective-permute-start.13) | collective-permute-done | bytes 81952 | tf_op jit(solution)/shard_map/ppermute | solution.py:401
  61.5 1.6 %collective-permute-start.14 = (bf16[160,256]{1,0:T(8,128)(2,1)S(1)}, bf16[160,256]{1,0:T(8,128)(2,1)S(1)}, u32[]{:S(2)}, u32[]{:S(2)}) collective-permute-start(bf16[160,256]{1,0:T(8,128)(2,1)S(1)} %add_parts.5.refs_0_), channel_id=1, source_target_pairs={{0,16},{16,0},{1,17},{17,1},{2,18},{18,2},{3,19},{19,3},{4,20},{20... | collective-permute-start | bytes 245768 | tf_op jit(solution)/shard_map/ppermute | solution.py:405
  63.1 2.9 %collective-permute-done.14.refs_1_ = bf16[160,256]{1,0:T(8,128)(2,1)S(1)} collective-permute-done((bf16[160,256]{1,0:T(8,128)(2,1)S(1)}, bf16[160,256]{1,0:T(8,128)(2,1)S(1)}, u32[]{:S(2)}, u32[]{:S(2)}) %collective-permute-start.14) | collective-permute-done | bytes 81952 | tf_op jit(solution)/shard_map/ppermute | solution.py:405
  66.0 1.0 %collective-permute-start.15 = (bf16[160,256]{1,0:T(8,128)(2,1)S(1)}, bf16[160,256]{1,0:T(8,128)(2,1)S(1)}, u32[]{:S(2)}, u32[]{:S(2)}) collective-permute-start(bf16[160,256]{1,0:T(8,128)(2,1)S(1)} %add_parts.6.refs_0_), channel_id=1, source_target_pairs={{0,1},{1,2},{2,3},{3,0},{4,5},{5,6},{6,7},{7,4},{8,9},{9,10},{10,1... | collective-permute-start | bytes 245768 | tf_op jit(solution)/shard_map/ppermute | solution.py:405
  67.1 3.5 %collective-permute-start.16 = (bf16[160,256]{1,0:T(8,128)(2,1)S(1)}, bf16[160,256]{1,0:T(8,128)(2,1)S(1)}, u32[]{:S(2)}, u32[]{:S(2)}) collective-permute-start(bf16[160,256]{1,0:T(8,128)(2,1)S(1)} %add_parts.6.refs_0_), channel_id=1, source_target_pairs={{0,2},{1,3},{2,0},{3,1},{4,6},{5,7},{6,4},{7,5},{8,10},{9,11},{10,... | collective-permute-start | bytes 245768 | tf_op jit(solution)/shard_map/ppermute | solution.py:405
  70.6 1.2 %collective-permute-start.17 = (bf16[160,256]{1,0:T(8,128)(2,1)S(1)}, bf16[160,256]{1,0:T(8,128)(2,1)S(1)}, u32[]{:S(2)}, u32[]{:S(2)}) collective-permute-start(bf16[160,256]{1,0:T(8,128)(2,1)S(1)} %add_parts.6.refs_0_), channel_id=1, source_target_pairs={{0,3},{1,0},{2,1},{3,2},{4,7},{5,4},{6,5},{7,6},{8,11},{9,8},{10,9... | collective-permute-start | bytes 245768 | tf_op jit(solution)/shard_map/ppermute | solution.py:405
  71.7 1.2 %collective-permute-done.15.refs_1_ = bf16[160,256]{1,0:T(8,128)(2,1)S(1)} collective-permute-done((bf16[160,256]{1,0:T(8,128)(2,1)S(1)}, bf16[160,256]{1,0:T(8,128)(2,1)S(1)}, u32[]{:S(2)}, u32[]{:S(2)}) %collective-permute-start.15) | collective-permute-done | bytes 81952 | tf_op jit(solution)/shard_map/ppermute | solution.py:405
  72.9 2.4 %collective-permute-done.16.refs_2_ = bf16[160,256]{1,0:T(8,128)(2,1)S(1)} collective-permute-done((bf16[160,256]{1,0:T(8,128)(2,1)S(1)}, bf16[160,256]{1,0:T(8,128)(2,1)S(1)}, u32[]{:S(2)}, u32[]{:S(2)}) %collective-permute-start.16) | collective-permute-done | bytes 81952 | tf_op jit(solution)/shard_map/ppermute | solution.py:405
  75.2 0.4 collective-permute-done.17.refs_3_
  75.7 0.4 collective-permute-start.18
  76.0 4.1 %collective-permute-done.18.other_ref = bf16[160,256]{1,0:T(8,128)(2,1)S(1)} collective-permute-done((bf16[160,256]{1,0:T(8,128)(2,1)S(1)}, bf16[160,256]{1,0:T(8,128)(2,1)S(1)}, u32[]{:S(2)}, u32[]{:S(2)}) %collective-permute-start.18) | collective-permute-done | bytes 81952 | tf_op jit(solution)/shard_map/ppermute | solution.py:401
  80.2 0.1 collective-permute-start.19
  80.3 0.5 collective-permute-start.8
  80.8 0.7 collective-permute-start.9
  81.4 1.0 %collective-permute-start.10 = (bf16[224,128]{1,0:T(8,128)(2,1)S(1)}, bf16[224,128]{1,0:T(8,128)(2,1)S(1)}, u32[]{:S(2)}, u32[]{:S(2)}) collective-permute-start(bf16[224,128]{1,0:T(8,128)(2,1)S(1)} %get-tuple-element.134), channel_id=1, source_target_pairs={{0,1},{1,2},{2,3},{3,0},{4,5},{5,6},{6,7},{7,4},{8,9},{9,10},{10,1... | collective-permute-start | bytes 172040 | tf_op jit(solution)/shard_map/ppermute | solution.py:589
  82.5 2.9 %collective-permute-start.11 = (bf16[224,128]{1,0:T(8,128)(2,1)S(1)}, bf16[224,128]{1,0:T(8,128)(2,1)S(1)}, u32[]{:S(2)}, u32[]{:S(2)}) collective-permute-start(bf16[224,128]{1,0:T(8,128)(2,1)S(1)} %get-tuple-element.134), channel_id=1, source_target_pairs={{0,3},{1,0},{2,1},{3,2},{4,7},{5,4},{6,5},{7,6},{8,11},{9,8},{10,9... | collective-permute-start | bytes 172040 | tf_op jit(solution)/shard_map/ppermute | solution.py:590
  85.3 2.3 %collective-permute-done.10.left_ref = bf16[224,128]{1,0:T(8,128)(2,1)S(1)} collective-permute-done((bf16[224,128]{1,0:T(8,128)(2,1)S(1)}, bf16[224,128]{1,0:T(8,128)(2,1)S(1)}, u32[]{:S(2)}, u32[]{:S(2)}) %collective-permute-start.10) | collective-permute-done | bytes 57376 | tf_op jit(solution)/shard_map/ppermute | solution.py:589
  87.6 3.4 %final.2.refs_0_ = bf16[2,222,32,128]{3,2,1,0:T(8,128)(2,1)} custom-call(f32[2,32,224,128]{3,2,1,0:T(8,128)S(1)} %get-tuple-element.131.g_ref, bf16[2,224,128]{2,1,0:T(8,128)(2,1)S(1)} %collective-permute-done.8.first_ref, bf16[2,224,128]{2,1,0:T(8,128)(2,1)S(1)} %collective-permute-done.9.second_ref, bf16[224,128]{1,0:T(8,128)(2,1)S(1)} %collective-permute-done.10.left_ref, ...), custom_call_target="tpu_custom_call" | custom-call | tf_op jit(solution)/shard_map/final/pallas_call | solution.py:596
  91.0 3.4 %final.3 = bf16[2,222,32,128]{3,2,1,0:T(8,128)(2,1)} custom-call(f32[2,32,224,128]{3,2,1,0:T(8,128)S(1)} %get-tuple-element.131.g_ref, bf16[2,224,128]{2,1,0:T(8,128)(2,1)S(1)} %collective-permute-done.8.first_ref, bf16[2,224,128]{2,1,0:T(8,128)(2,1)S(1)} %collective-permute-done.9.second_ref, ...), custom_call_target="tpu_custom_call", output_to_operand_aliasing={{}: (6, {})} | custom-call | tf_op jit(solution)/shard_map/final/pallas_call | solution.py:596
  94.4 1.0 %unpack.1 = (f32[222,256]{1,0:T(8,128)}, f32[16,256]{1,0:T(8,128)}, f32[256,256]{1,0:T(8,128)}, f32[222,256]{1,0:T(8,128)}, f32[1,222]{1,0:T(1,128)}) custom-call(bf16[320,256]{1,0:T(8,128)(2,1)S(1)} %join_halves.1.mine_ref, bf16[320,256]{1,0:T(8,128)(2,1)S(1)} %collective-permute-done.19.other_ref, bf16[240,222]{1,0:T(8,128)(2,1)S(1)} %copy-done.1, ...), custom_call_target="tpu_custom_call" | custom-call | tf_op jit(solution)/shard_map/unpack/pallas_call | solution.py:632
  (16 shorter events, 0.1 us)
Async XLA Ops:
  7.8 18.0 %collective-permute-start = (bf16[2,224,128]{2,1,0:T(8,128)(2,1)S(1)}, bf16[2,224,128]{2,1,0:T(8,128)(2,1)S(1)}, u32[]{:S(2)}, u32[]{:S(2)}) collective-permute-start(bf16[2,224,128]{2,1,0:T(8,128)(2,1)S(1)} %get-tuple-element.76), channel_id=1, source_target_pairs={{0,4},{8,12},{4,0},{12,8},{1,5},{9,13},{5,1},{13,9},{2,6},{10,14},... | collective-permute-start | bytes 344072 | tf_op jit(solution)/shard_map/ppermute | solution.py:397
  8.4 17.5 %collective-permute-start.1 = (bf16[2,224,128]{2,1,0:T(8,128)(2,1)S(1)}, bf16[2,224,128]{2,1,0:T(8,128)(2,1)S(1)}, u32[]{:S(2)}, u32[]{:S(2)}) collective-permute-start(bf16[2,224,128]{2,1,0:T(8,128)(2,1)S(1)} %get-tuple-element.77), channel_id=1, source_target_pairs={{4,8},{8,4},{5,9},{9,5},{6,10},{10,6},{7,11},{11,7},{20,24},{24,20... | collective-permute-start | bytes 344072 | tf_op jit(solution)/shard_map/ppermute | solution.py:397
  9.0 6.9 %collective-permute-start.2 = (bf16[224,128]{1,0:T(8,128)(2,1)S(1)}, bf16[224,128]{1,0:T(8,128)(2,1)S(1)}, u32[]{:S(2)}, u32[]{:S(2)}) collective-permute-start(bf16[224,128]{1,0:T(8,128)(2,1)S(1)} %get-tuple-element.78), channel_id=1, source_target_pairs={{0,1},{1,2},{2,3},{3,0},{4,5},{5,6},{6,7},{7,4},{8,9},{9,10},{10,1... | collective-permute-start | bytes 172040 | tf_op jit(solution)/shard_map/ppermute | solution.py:500
  11.7 4.8 %collective-permute-start.3 = (bf16[224,128]{1,0:T(8,128)(2,1)S(1)}, bf16[224,128]{1,0:T(8,128)(2,1)S(1)}, u32[]{:S(2)}, u32[]{:S(2)}) collective-permute-start(bf16[224,128]{1,0:T(8,128)(2,1)S(1)} %get-tuple-element.78), channel_id=1, source_target_pairs={{0,3},{1,0},{2,1},{3,2},{4,7},{5,4},{6,5},{7,6},{8,11},{9,8},{10,9... | collective-permute-start | bytes 172040 | tf_op jit(solution)/shard_map/ppermute | solution.py:500
  20.1 15.6 %collective-permute-start.7 = (bf16[2,8,80,128]{3,2,1,0:T(8,128)(2,1)S(1)}, bf16[2,8,80,128]{3,2,1,0:T(8,128)(2,1)S(1)}, u32[]{:S(2)}, u32[]{:S(2)}) collective-permute-start(bf16[2,8,80,128]{3,2,1,0:T(8,128)(2,1)S(1)} %get-tuple-element.106.own_ref), channel_id=1, source_target_pairs={{0,16},{16,0},{1,17},{17,1},{2,18},{18,2},{3,19},{19,3},{4,20},{20... | collective-permute-start | bytes 983048 | tf_op jit(solution)/shard_map/ppermute | solution.py:580
  25.2 10.0 %copy-start = (f32[6,13,32,128]{3,2,1,0:T(8,128)S(1)}, f32[6,13,32,128]{3,2,1,0:T(8,128)}, u32[]{:S(2)}) copy-start(f32[6,13,32,128]{3,2,1,0:T(8,128)} %param.14) | copy-start | bytes 3833860
  25.2 13.4 %collective-permute-start.6 = (bf16[2,8,80,128]{3,2,1,0:T(8,128)(2,1)S(1)}, bf16[2,8,80,128]{3,2,1,0:T(8,128)(2,1)S(1)}, u32[]{:S(2)}, u32[]{:S(2)}) collective-permute-start(bf16[2,8,80,128]{3,2,1,0:T(8,128)(2,1)S(1)} %get-tuple-element.99.own_ref), channel_id=1, source_target_pairs={{0,16},{16,0},{1,17},{17,1},{2,18},{18,2},{3,19},{19,3},{4,20},{20... | collective-permute-start | bytes 983048 | tf_op jit(solution)/shard_map/ppermute | solution.py:580
  29.4 14.3 %collective-permute-start.5 = (bf16[2,8,80,128]{3,2,1,0:T(8,128)(2,1)S(1)}, bf16[2,8,80,128]{3,2,1,0:T(8,128)(2,1)S(1)}, u32[]{:S(2)}, u32[]{:S(2)}) collective-permute-start(bf16[2,8,80,128]{3,2,1,0:T(8,128)(2,1)S(1)} %get-tuple-element.92.own_ref), channel_id=1, source_target_pairs={{0,16},{16,0},{1,17},{17,1},{2,18},{18,2},{3,19},{19,3},{4,20},{20... | collective-permute-start | bytes 983048 | tf_op jit(solution)/shard_map/ppermute | solution.py:580
  34.6 16.2 %collective-permute-start.4 = (bf16[2,8,80,128]{3,2,1,0:T(8,128)(2,1)S(1)}, bf16[2,8,80,128]{3,2,1,0:T(8,128)(2,1)S(1)}, u32[]{:S(2)}, u32[]{:S(2)}) collective-permute-start(bf16[2,8,80,128]{3,2,1,0:T(8,128)(2,1)S(1)} %get-tuple-element.83.own_ref), channel_id=1, source_target_pairs={{0,16},{16,0},{1,17},{17,1},{2,18},{18,2},{3,19},{19,3},{4,20},{20... | collective-permute-start | bytes 983048 | tf_op jit(solution)/shard_map/ppermute | solution.py:580
  54.8 1.8 %collective-permute-start.12 = (bf16[320,256]{1,0:T(8,128)(2,1)S(1)}, bf16[320,256]{1,0:T(8,128)(2,1)S(1)}, u32[]{:S(2)}, u32[]{:S(2)}) collective-permute-start(bf16[320,256]{1,0:T(8,128)(2,1)S(1)} %get-tuple-element.136), channel_id=1, source_target_pairs={{0,4},{4,0},{8,12},{12,8},{1,5},{5,1},{9,13},{13,9},{2,6},{6,2},{1... | collective-permute-start | bytes 491528 | tf_op jit(solution)/shard_map/ppermute | solution.py:401
  56.7 4.8 %collective-permute-start.13 = (bf16[160,256]{1,0:T(8,128)(2,1)S(1)}, bf16[160,256]{1,0:T(8,128)(2,1)S(1)}, u32[]{:S(2)}, u32[]{:S(2)}) collective-permute-start(bf16[160,256]{1,0:T(8,128)(2,1)S(1)} %get-tuple-element.138), channel_id=1, source_target_pairs={{0,8},{4,12},{8,0},{12,4},{1,9},{5,13},{9,1},{13,5},{2,10},{6,14},... | collective-permute-start | bytes 245768 | tf_op jit(solution)/shard_map/ppermute | solution.py:401
  61.5 4.5 %collective-permute-start.14 = (bf16[160,256]{1,0:T(8,128)(2,1)S(1)}, bf16[160,256]{1,0:T(8,128)(2,1)S(1)}, u32[]{:S(2)}, u32[]{:S(2)}) collective-permute-start(bf16[160,256]{1,0:T(8,128)(2,1)S(1)} %add_parts.5.refs_0_), channel_id=1, source_target_pairs={{0,16},{16,0},{1,17},{17,1},{2,18},{18,2},{3,19},{19,3},{4,20},{20... | collective-permute-start | bytes 245768 | tf_op jit(solution)/shard_map/ppermute | solution.py:405
  66.0 6.8 %collective-permute-start.15 = (bf16[160,256]{1,0:T(8,128)(2,1)S(1)}, bf16[160,256]{1,0:T(8,128)(2,1)S(1)}, u32[]{:S(2)}, u32[]{:S(2)}) collective-permute-start(bf16[160,256]{1,0:T(8,128)(2,1)S(1)} %add_parts.6.refs_0_), channel_id=1, source_target_pairs={{0,1},{1,2},{2,3},{3,0},{4,5},{5,6},{6,7},{7,4},{8,9},{9,10},{10,1... | collective-permute-start | bytes 245768 | tf_op jit(solution)/shard_map/ppermute | solution.py:405
  67.1 8.2 %collective-permute-start.16 = (bf16[160,256]{1,0:T(8,128)(2,1)S(1)}, bf16[160,256]{1,0:T(8,128)(2,1)S(1)}, u32[]{:S(2)}, u32[]{:S(2)}) collective-permute-start(bf16[160,256]{1,0:T(8,128)(2,1)S(1)} %add_parts.6.refs_0_), channel_id=1, source_target_pairs={{0,2},{1,3},{2,0},{3,1},{4,6},{5,7},{6,4},{7,5},{8,10},{9,11},{10,... | collective-permute-start | bytes 245768 | tf_op jit(solution)/shard_map/ppermute | solution.py:405
  70.6 5.0 %collective-permute-start.17 = (bf16[160,256]{1,0:T(8,128)(2,1)S(1)}, bf16[160,256]{1,0:T(8,128)(2,1)S(1)}, u32[]{:S(2)}, u32[]{:S(2)}) collective-permute-start(bf16[160,256]{1,0:T(8,128)(2,1)S(1)} %add_parts.6.refs_0_), channel_id=1, source_target_pairs={{0,3},{1,0},{2,1},{3,2},{4,7},{5,4},{6,5},{7,6},{8,11},{9,8},{10,9... | collective-permute-start | bytes 245768 | tf_op jit(solution)/shard_map/ppermute | solution.py:405
  75.7 4.5 %collective-permute-start.18 = (bf16[160,256]{1,0:T(8,128)(2,1)S(1)}, bf16[160,256]{1,0:T(8,128)(2,1)S(1)}, u32[]{:S(2)}, u32[]{:S(2)}) collective-permute-start(bf16[160,256]{1,0:T(8,128)(2,1)S(1)} %add_parts.7.mine_ref), channel_id=1, source_target_pairs={{0,8},{4,12},{8,0},{12,4},{1,9},{5,13},{9,1},{13,5},{2,10},{6,14},... | collective-permute-start | bytes 245768 | tf_op jit(solution)/shard_map/ppermute | solution.py:401
  80.2 14.2 %collective-permute-start.19 = (bf16[320,256]{1,0:T(8,128)(2,1)S(1)}, bf16[320,256]{1,0:T(8,128)(2,1)S(1)}, u32[]{:S(2)}, u32[]{:S(2)}) collective-permute-start(bf16[320,256]{1,0:T(8,128)(2,1)S(1)} %join_halves.1.mine_ref), channel_id=1, source_target_pairs={{0,4},{4,0},{8,12},{12,8},{1,5},{5,1},{9,13},{13,9},{2,6},{6,2},{1... | collective-permute-start | bytes 491528 | tf_op jit(solution)/shard_map/ppermute | solution.py:401
  80.3 7.3 %collective-permute-start.8 = (bf16[2,224,128]{2,1,0:T(8,128)(2,1)S(1)}, bf16[2,224,128]{2,1,0:T(8,128)(2,1)S(1)}, u32[]{:S(2)}, u32[]{:S(2)}) collective-permute-start(bf16[2,224,128]{2,1,0:T(8,128)(2,1)S(1)} %get-tuple-element.132), channel_id=1, source_target_pairs={{0,4},{8,12},{4,0},{12,8},{1,5},{9,13},{5,1},{13,9},{2,6},{10,14},... | collective-permute-start | bytes 344072 | tf_op jit(solution)/shard_map/ppermute | solution.py:397
  80.8 6.8 %collective-permute-start.9 = (bf16[2,224,128]{2,1,0:T(8,128)(2,1)S(1)}, bf16[2,224,128]{2,1,0:T(8,128)(2,1)S(1)}, u32[]{:S(2)}, u32[]{:S(2)}) collective-permute-start(bf16[2,224,128]{2,1,0:T(8,128)(2,1)S(1)} %get-tuple-element.133), channel_id=1, source_target_pairs={{4,8},{8,4},{5,9},{9,5},{6,10},{10,6},{7,11},{11,7},{20,24},{24,20... | collective-permute-start | bytes 344072 | tf_op jit(solution)/shard_map/ppermute | solution.py:397
  81.4 6.1 %collective-permute-start.10 = (bf16[224,128]{1,0:T(8,128)(2,1)S(1)}, bf16[224,128]{1,0:T(8,128)(2,1)S(1)}, u32[]{:S(2)}, u32[]{:S(2)}) collective-permute-start(bf16[224,128]{1,0:T(8,128)(2,1)S(1)} %get-tuple-element.134), channel_id=1, source_target_pairs={{0,1},{1,2},{2,3},{3,0},{4,5},{5,6},{6,7},{7,4},{8,9},{9,10},{10,1... | collective-permute-start | bytes 172040 | tf_op jit(solution)/shard_map/ppermute | solution.py:589
  82.5 5.1 %collective-permute-start.11 = (bf16[224,128]{1,0:T(8,128)(2,1)S(1)}, bf16[224,128]{1,0:T(8,128)(2,1)S(1)}, u32[]{:S(2)}, u32[]{:S(2)}) collective-permute-start(bf16[224,128]{1,0:T(8,128)(2,1)S(1)} %get-tuple-element.134), channel_id=1, source_target_pairs={{0,3},{1,0},{2,1},{3,2},{4,7},{5,4},{6,5},{7,6},{8,11},{9,8},{10,9... | collective-permute-start | bytes 172040 | tf_op jit(solution)/shard_map/ppermute | solution.py:590
  91.0 3.4 %copy-start.1 = (bf16[240,222]{1,0:T(8,128)(2,1)S(1)}, bf16[240,222]{1,0:T(8,128)(2,1)}, u32[]{:S(2)}) copy-start(bf16[240,222]{1,0:T(8,128)(2,1)} %constant.8.clone.refs_5_.place_ref) | copy-start | bytes 319684
  91.0 3.4 %copy-start.2 = (bf16[222,80]{1,0:T(8,128)(2,1)S(1)}, bf16[222,80]{1,0:T(8,128)(2,1)}, u32[]{:S(2)}) copy-start(bf16[222,80]{1,0:T(8,128)(2,1)} %constant.10.clone.refs_7_.scat_ref) | copy-start | bytes 106564
where the time goes:
time: 96 us; the launch traced here: 95.4 us
  Pallas kernels  43 us (45%)
  waiting for transfers between devices  27.4 us (29%)
  starting transfers between devices  24.2 us (25%)
    pallas_call x4, Pallas kernels, forward(): pl.pallas_call(body, in_specs=[RESIDENT] * (7 + len(halo)), out_specs=[RE...  14.4 us
    pallas_call x4, Pallas kernels, backward(): pl.pallas_call(functools.partial(backward_kernel, partners, first, last,...  13 us
    ppermute x4, waiting for transfers between devices, across(): lax.ppermute(value, 'lat', [(i, i ^ bit) for i in range(lax.axis_size('la...  9.5 us
    ppermute x4, starting transfers between devices, everyone(): lax.ppermute(value, axis, ring(axis, k))  7.24 us
    pallas_call x1, Pallas kernels, on_device(): pl.pallas_call(functools.partial(transpose_kernel, order, channels, len(s...  7.17 us
    ppermute x4, waiting for transfers between devices, everyone(): lax.ppermute(value, axis, ring(axis, k))  6.82 us
    pallas_call x2, Pallas kernels, final(): pl.pallas_call(functools.partial(final_kernel, order, span, chunk, first,...  6.77 us
    ppermute x4, waiting for transfers between devices, on_device(): lax.ppermute(saved[index][0], 'ens', ring('ens', k))  6.15 us
  transfers between devices with their start and end apart: 20, of which 12 were waited for; matrix products, arithmetic and copies ran while one was open for 0% of the time, Pallas kernels for 32%

commit v1 on v0

--- a/solution.py
+++ b/solution.py
@@ -165,12 +165,11 @@
 
 
 def forward_kernel(
-    first_row, rows, scored, member_span, t_ref, up_ref, dn_ref, left_ref, right_ref, coef_ref, win_ref, wmid_ref,
-    wout_ref, f_ref, x_ref, lap_ref, act1_ref, slope1_ref, act2_ref, slope2_ref, keep, around, weights,
+    first_row, rows, scored, member_span, t_ref, up_ref, dn_ref, around, weights, coef_ref, win_ref, wmid_ref,
+    wout_ref, f_ref, x_ref, lap_ref, act1_ref, slope1_ref, act2_ref, slope2_ref, keep,
 ):
     state_rows, lanes = coef_ref.shape
     kept = keep.shape[0]
-    stencil_setup(left_ref, right_ref, around, weights)
     even = lax.axis_index("lat") % 2 == 0
 
     def member(m, _):
@@ -209,7 +208,7 @@
                 f_ref[m, at // lanes + j] = jnp.where(scored_row, piece, 0.0).astype(BF16)
         return 0
 
-    lax.fori_loop(0, t_ref.shape[0], member, 0)
+    lax.fori_loop(0, t_ref.shape[0], member, 0, unroll=rows < SUB)
 
 
 def backward_kernel(
@@ -285,8 +284,7 @@
     lax.fori_loop(0, chunk_rows // rows, part, 0)
     edge_out[...] = edge[...].astype(BF16)
     if last:
-        low = grad_ref[:, 0] if first else in_refs[5][:, 0]
-        choose_rows(low, grad_ref[:, first_row + chunk_rows - 1], first_ref, second_ref)
+        choose_rows(in_refs[5][:, 0], in_refs[5][:, grad_ref.shape[1] - 1], first_ref, second_ref)
         pack_ref, part_refs = part_refs[-1], part_refs[:-1]
         at = 0
         for acc in (in_acc, mid_acc, out_acc):
@@ -444,9 +442,6 @@
     span = 2 * lat_rows
     order = channel_order()
     blocks = lat_rows // SUB
-    chunk = SUB
-    chunks = lat_rows // chunk
-    cells = chunk * lanes
     partners = lax.axis_size("ens") - 1
     assert members * span <= lanes and lat_rows % SUB == 0
     lat_n, lon_n = lax.axis_size("lat"), lax.axis_size("lon")
@@ -509,39 +504,48 @@
         name="observed",
     )(in_vmem(observed.reshape(scored, lat_rows, lanes)))
 
-    def forward(index, swapped):
-        first_row = index * chunk
-        at_start, at_end = index == 0, index == chunks - 1
+    half = SUB // 2
+    inner = [(at, SUB) for at in range(SUB, lat_rows - SUB, SUB)]
+    pieces = [*inner, (0, SUB), (lat_rows - half, half), (lat_rows - SUB, half)]
+
+    def forward(index, swapped, sides):
+        first_row, chunk = pieces[index]
+        cells = chunk * lanes
+        at_start, at_end = first_row == 0, first_row + chunk == lat_rows
         halo = list(swapped) if at_start or at_end else []
 
         def body(t_ref, *refs):
             got, refs = refs[: len(halo)], refs[len(halo) :]
             up, down = got if at_start else None, got if at_end else None
-            forward_kernel(first_row, chunk, scored, span, t_ref, up, down, *refs)
+            around, weights, *refs = refs
+            if index == 0:
+                left, right, (around, weights, keep) = around, weights, refs[-3:]
+                stencil_setup(left, right, around, weights)
+                refs = [*refs[:-3], keep]
+            forward_kernel(first_row, chunk, scored, span, t_ref, up, down, around, weights, *refs)
 
         return pl.pallas_call(
             body,
             in_specs=[RESIDENT] * (7 + len(halo)),
-            out_specs=[RESIDENT] * 7,
+            out_specs=[RESIDENT] * (9 if index == 0 else 7),
             out_shape=[
                 pltpu.VMEM((members, chunk, kept, lanes), BF16),
                 pltpu.VMEM((members, total, cells), BF16),
                 pltpu.VMEM((members, chunk, state_rows, lanes), BF16),
                 *[pltpu.VMEM((members, hidden, cells), BF16) for _ in range(4)],
+                *([pltpu.VMEM((state_rows, lanes), F32)] if index == 0 else []),
+                *([pltpu.VMEM((2 * lanes, lanes), BF16)] if index == 0 else []),
             ],
-            scratch_shapes=[
-                pltpu.VMEM((kept, cells), F32),
-                pltpu.VMEM((state_rows, lanes), F32),
-                pltpu.VMEM((2 * lanes, lanes), BF16),
-            ],
+            scratch_shapes=[pltpu.VMEM((kept, cells), F32)],
             compiler_params=params(),
-        )(in_vmem(rows_t), *halo, *sides, coef, w_in_half, w_mid_half, w_out)
+        )(in_vmem(rows_t), *halo, *map(in_vmem, sides), coef, w_in_half, w_mid_half, w_out)
 
     pack_rows = round_up(total + hidden + kept + 8, 16 * lat_n)
 
     def backward(index, residuals, others, carried, grads):
         own, x, lap, act1, slope1, act2, slope2 = residuals
-        first, last = index == chunk_order[0], index == chunk_order[-1]
+        first, last = index == 0, index == len(pieces) - 1
+        first_row = pieces[index][0]
         rows = 4
         accs = [(total, hidden), (hidden, hidden), (kept, hidden), (state_rows, lanes), (state_rows, lanes)]
         acc_types = [F32, F32, F32, F32, BF16]
@@ -556,7 +560,7 @@
             *([pltpu.VMEM((pack_rows // 2, hidden), BF16)] * 2 if last else []),
         ]
         return pl.pallas_call(
-            functools.partial(backward_kernel, partners, first, last, index * chunk, span),
+            functools.partial(backward_kernel, partners, first, last, first_row, span),
             in_specs=[RESIDENT] * len(inputs),
             out_specs=[RESIDENT] * len(outputs),
             out_shape=outputs,
@@ -569,18 +573,20 @@
             compiler_params=params(),
         )(*inputs)
 
-    chunk_order = [*range(1, chunks - 1), 0, chunks - 1] if chunks > 1 else [0]
     saved, received = {}, {}
     swapped = None
-    for index in chunk_order:
+    for index in range(len(pieces)):
+        if index == len(inner):
+            swapped = swap(low, 0), swap(high, 1)
+        saved[index] = forward(index, swapped, sides)
         if index == 0:
-            swapped = swap(low, 0), swap(high, 1)
-        saved[index] = forward(index, swapped)
+            *saved[index], around, turned = saved[index]
+            sides = around, turned
         received[index] = [
             lax.ppermute(saved[index][0], "ens", ring("ens", k)) for k in range(1, partners + 1)
         ]
     grads, carried = None, []
-    for index in chunk_order:
+    for index in range(len(pieces)):
         grads, *carried = backward(index, saved[index], received[index], carried, grads)
         carried, more = carried[:5], carried[5:]
     edge, (low, high, mine, other) = carried[-1], more
@@ -591,16 +597,16 @@
 
     def final(which, out):
         inputs = [*map(in_vmem, (grads, *swapped, *sides)), coef]
-        first, stride = which[0], which[-1] - which[0]
+        first, stride = which[0], which[1] - which[0]
         index_map = lambda m, j: (m, 0, first + j * stride, 0)
         return pl.pallas_call(
-            functools.partial(final_kernel, order, span, chunk, first, stride, chunks),
+            functools.partial(final_kernel, order, span, SUB, first, stride, blocks),
             grid=(members, len(which)),
             in_specs=[
                 *[RESIDENT] * len(inputs),
                 *([] if out is None else [pl.BlockSpec(memory_space=pl.ANY)]),
             ],
-            out_specs=pl.BlockSpec((1, channels, chunk, lanes), index_map),
+            out_specs=pl.BlockSpec((1, channels, SUB, lanes), index_map),
             out_shape=pltpu.HBM(starting_state.shape, BF16),
             scratch_shapes=[
                 pltpu.VMEM((state_rows * SUB, lanes), F32),
@@ -620,14 +626,14 @@
     parts = everyone(mine, "ens")
     (mine,) = add_parts(parts)
     parts = everyone(mine, "lon")
-    grad_state = final(chunk_order[:-2], None)
+    grad_state = final(range(1, blocks - 1), None)
     (mine,) = add_parts(parts)
     for bit in bits[::-1]:
         other = across(mine, bit)
         if bit != bits[0]:
             mine = join(bit, mine, other)
     parts = [mine, other]
-    grad_state = final(chunk_order[-2:], grad_state)
+    grad_state = final((0, blocks - 1), grad_state)
     count = members * (partners + 1) * lat_rows * lat_n * lanes * lon_n
     g_in, g_noise, g_mid, g_out, g_diff = pl.pallas_call(
         functools.partial(unpack_kernel, channels, noise, 1.0 / count),

time: 96 us -> 95.5 us (level)
  starting transfers between devices: 24.2 us -> 27.3 us
  waiting for transfers between devices: 27.4 us -> 24.7 us
    ppermute x4 -> x5, waiting for transfers between devices: 6.15 us -> 3.38 us  [on_device(): lax.ppermute(saved[index][0], 'ens', ring('ens', k))]
    ppermute x4 -> x5, starting transfers between devices: 4.31 us -> 5.89 us  [on_device(): lax.ppermute(saved[index][0], 'ens', ring('ens', k))]
    ppermute x4, starting transfers between devices: 2.37 us -> 3.72 us  [swap(): return lax.ppermute(value, 'lat', [*pairs, *((b, a) for a, b in pairs)])]
    pallas_call x4 -> x5, Pallas kernels: 14.4 us -> 14 us  [forward(): pl.pallas_call(body, in_specs=[RESIDENT] * (7 + len(halo)), out_specs=[RE...]
    pallas_call x4 -> x5, Pallas kernels: 13 us -> 12.9 us  [backward(): pl.pallas_call(functools.partial(backward_kernel, partners, first, last,...]
  transfers between devices with their start and end apart: 20 -> 21, of which waited for: 12 -> 13; matrix products, arithmetic and copies ran while one was open for 0% -> 0% of each run, Pallas kernels for 32% -> 33%
where the time goes in v1:
time: 95.5 us; the launch traced here: 95.3 us
  Pallas kernels  42.4 us (44%)
  starting transfers between devices  27.3 us (29%)
  waiting for transfers between devices  24.7 us (26%)
    pallas_call x5, Pallas kernels, forward(): pl.pallas_call(body, in_specs=[RESIDENT] * (7 + len(halo)), out_specs=[RE...  14 us
    pallas_call x5, Pallas kernels, backward(): pl.pallas_call(functools.partial(backward_kernel, partners, first, last,...  12.9 us
    ppermute x4, waiting for transfers between devices, across(): lax.ppermute(value, 'lat', [(i, i ^ bit) for i in range(lax.axis_size('la...  9.24 us
    ppermute x4, starting transfers between devices, everyone(): lax.ppermute(value, axis, ring(axis, k))  7.23 us
    pallas_call x1, Pallas kernels, on_device(): pl.pallas_call(functools.partial(transpose_kernel, order, channels, len(s...  7.17 us
    ppermute x4, waiting for transfers between devices, everyone(): lax.ppermute(value, axis, ring(axis, k))  6.81 us
    pallas_call x2, Pallas kernels, final(): pl.pallas_call(functools.partial(final_kernel, order, span, SUB, first, s...  6.75 us
    ppermute x5, starting transfers between devices, on_device(): lax.ppermute(saved[index][0], 'ens', ring('ens', k))  5.89 us
  transfers between devices with their start and end apart: 21, of which 13 were waited for; matrix products, arithmetic and copies ran while one was open for 0% of the time, Pallas kernels for 33%

profile of v1, /device:TPU:0, one launch (start us, length us, event | category | flops | bytes accessed | tf_op | source)
XLA Modules:
  0.0 95.3 jit_solution(6324199704806804350)
XLA Ops:
  0.6 7.2 %transpose.17 = (f32[2,32,240,128]{3,2,1,0:T(8,128)S(1)}, bf16[2,224,128]{2,1,0:T(8,128)(2,1)S(1)}, bf16[2,224,128]{2,1,0:T(8,128)(2,1)S(1)}, bf16[224,128]{1,0:...) custom-call(bf16[2,222,32,128]{3,2,1,0:T(8,128)(2,1)} %st_ref.1, ...), custom_call_target="tpu_custom_call" | custom-call | tf_op jit(solution)/shard_map/transpose/pallas_call | solution.py:467
  7.8 0.6 collective-permute-start.3
  8.4 0.7 collective-permute-start.4
  9.0 2.6 %collective-permute-start = (bf16[224,128]{1,0:T(8,128)(2,1)S(1)}, bf16[224,128]{1,0:T(8,128)(2,1)S(1)}, u32[]{:S(2)}, u32[]{:S(2)}) collective-permute-start(bf16[224,128]{1,0:T(8,128)(2,1)S(1)} %get-tuple-element.91), channel_id=1, source_target_pairs={{0,1},{1,2},{2,3},{3,0},{4,5},{5,6},{6,7},{7,4},{8,9},{9,10},{10,1... | collective-permute-start | bytes 172040 | tf_op jit(solution)/shard_map/ppermute | solution.py:495
  11.7 2.1 %collective-permute-start.1 = (bf16[224,128]{1,0:T(8,128)(2,1)S(1)}, bf16[224,128]{1,0:T(8,128)(2,1)S(1)}, u32[]{:S(2)}, u32[]{:S(2)}) collective-permute-start(bf16[224,128]{1,0:T(8,128)(2,1)S(1)} %get-tuple-element.91), channel_id=1, source_target_pairs={{0,3},{1,0},{2,1},{3,2},{4,7},{5,4},{6,5},{7,6},{8,11},{9,8},{10,9... | collective-permute-start | bytes 172040 | tf_op jit(solution)/shard_map/ppermute | solution.py:495
  13.8 2.2 %collective-permute-done.refs_0_ = bf16[224,128]{1,0:T(8,128)(2,1)S(1)} collective-permute-done((bf16[224,128]{1,0:T(8,128)(2,1)S(1)}, bf16[224,128]{1,0:T(8,128)(2,1)S(1)}, u32[]{:S(2)}, u32[]{:S(2)}) %collective-permute-start) | collective-permute-done | bytes 57376 | tf_op jit(solution)/shard_map/ppermute | solution.py:495
  16.0 0.5 collective-permute-done.1.refs_1_
  16.5 3.6 %shard_map.163 = (bf16[2,8,80,128]{3,2,1,0:T(8,128)(2,1)S(1)}, bf16[2,240,1024]{2,1,0:T(8,128)(2,1)S(1)}, bf16[2,8,224,128]{3,2,1,0:T(8,128)(2,1)S(1)}, bf16[2,2...) custom-call(f32[2,32,240,128]{3,2,1,0:T(8,128)S(1)} %get-tuple-eleme, ...), custom_call_target="tpu_custom_call" | custom-call | tf_op jit(solution)/shard_map/pallas_call | solution.py:527
  20.1 1.6 %collective-permute-start.8 = (bf16[2,8,80,128]{3,2,1,0:T(8,128)(2,1)S(1)}, bf16[2,8,80,128]{3,2,1,0:T(8,128)(2,1)S(1)}, u32[]{:S(2)}, u32[]{:S(2)}) collective-permute-start(bf16[2,8,80,128]{3,2,1,0:T(8,128)(2,1)S(1)} %get-tuple-element.130.own_ref), channel_id=1, source_target_pairs={{0,16},{16,0},{1,17},{17,1},{2,18},{18,2},{3,19},{19,3},{4,20},{20... | collective-permute-start | bytes 983048 | tf_op jit(solution)/shard_map/ppermute | solution.py:586
  21.6 3.5 %shard_map.167 = (bf16[2,8,80,128]{3,2,1,0:T(8,128)(2,1)S(1)}, bf16[2,240,1024]{2,1,0:T(8,128)(2,1)S(1)}, bf16[2,8,224,128]{3,2,1,0:T(8,128)(2,1)S(1)}, bf16[2,2...) custom-call(f32[2,32,240,128]{3,2,1,0:T(8,128)S(1)} %get-tuple-eleme, ...), custom_call_target="tpu_custom_call" | custom-call | tf_op jit(solution)/shard_map/pallas_call | solution.py:527
  25.1 0.6 collective-permute-start.7
  25.7 3.5 %shard_map.166 = (bf16[2,8,80,128]{3,2,1,0:T(8,128)(2,1)S(1)}, bf16[2,240,1024]{2,1,0:T(8,128)(2,1)S(1)}, bf16[2,8,224,128]{3,2,1,0:T(8,128)(2,1)S(1)}, bf16[2,2...) custom-call(f32[2,32,240,128]{3,2,1,0:T(8,128)S(1)} %get-tuple-eleme, ...), custom_call_target="tpu_custom_call" | custom-call | tf_op jit(solution)/shard_map/pallas_call | solution.py:527
  29.2 1.6 %collective-permute-start.6 = (bf16[2,8,80,128]{3,2,1,0:T(8,128)(2,1)S(1)}, bf16[2,8,80,128]{3,2,1,0:T(8,128)(2,1)S(1)}, u32[]{:S(2)}, u32[]{:S(2)}) collective-permute-start(bf16[2,8,80,128]{3,2,1,0:T(8,128)(2,1)S(1)} %get-tuple-element.116.own_ref), channel_id=1, source_target_pairs={{0,16},{16,0},{1,17},{17,1},{2,18},{18,2},{3,19},{19,3},{4,20},{20... | collective-permute-start | bytes 983048 | tf_op jit(solution)/shard_map/ppermute | solution.py:586
  30.8 1.7 %shard_map.165 = (bf16[2,4,80,128]{3,2,1,0:T(8,128)(2,1)S(1)}, bf16[2,240,512]{2,1,0:T(8,128)(2,1)S(1)}, bf16[2,4,224,128]{3,2,1,0:T(8,128)(2,1)S(1)}, bf16[2,25...) custom-call(f32[2,32,240,128]{3,2,1,0:T(8,128)S(1)} %get-tuple-eleme, ...), custom_call_target="tpu_custom_call" | custom-call | tf_op jit(solution)/shard_map/pallas_call | solution.py:527
  32.5 0.6 collective-permute-start.5
  33.1 1.7 %shard_map.164 = (bf16[2,4,80,128]{3,2,1,0:T(8,128)(2,1)S(1)}, bf16[2,240,512]{2,1,0:T(8,128)(2,1)S(1)}, bf16[2,4,224,128]{3,2,1,0:T(8,128)(2,1)S(1)}, bf16[2,25...) custom-call(f32[2,32,240,128]{3,2,1,0:T(8,128)S(1)} %get-tuple-eleme, ...), custom_call_target="tpu_custom_call" | custom-call | tf_op jit(solution)/shard_map/pallas_call | solution.py:527
  34.8 1.6 %collective-permute-start.2 = (bf16[2,4,80,128]{3,2,1,0:T(8,128)(2,1)S(1)}, bf16[2,4,80,128]{3,2,1,0:T(8,128)(2,1)S(1)}, u32[]{:S(2)}, u32[]{:S(2)}) collective-permute-start(bf16[2,4,80,128]{3,2,1,0:T(8,128)(2,1)S(1)} %get-tuple-element.98.own_ref), channel_id=1, source_target_pairs={{0,16},{16,0},{1,17},{17,1},{2,18},{18,2},{3,19},{19,3},{4,20},{20... | collective-permute-start | bytes 491528 | tf_op jit(solution)/shard_map/ppermute | solution.py:586
  36.4 0.4 observed.1.refs_1_
  36.8 3.0 %shard_map.168 = (f32[2,32,224,128]{3,2,1,0:T(8,128)S(1)}, f32[240,256]{1,0:T(8,128)S(1)}, f32[256,256]{1,0:T(8,128)S(1)}, f32[80,256]{1,0:T(8,128)S(1)}, f32[22...) custom-call(bf16[2,8,80,128]{3,2,1,0:T(8,128)(2,1)S(1)} %get-tuple-element.130.own_ref, ...), custom_call_target="tpu_custom_call" | custom-call | tf_op jit(solution)/shard_map/pallas_call | solution.py:562
  39.8 3.0 %shard_map.169 = (f32[2,32,224,128]{3,2,1,0:T(8,128)S(1)}, f32[240,256]{1,0:T(8,128)S(1)}, f32[256,256]{1,0:T(8,128)S(1)}, f32[80,256]{1,0:T(8,128)S(1)}, f32[22...) custom-call(bf16[2,8,80,128]{3,2,1,0:T(8,128)(2,1)S(1)} %get-tuple-element.123.own_ref, ...), custom_call_target="tpu_custom_call", output_to_operand_aliasing={{0}: (17, {})} | custom-call | tf_op jit(solution)/shard_map/pallas_call | solution.py:562
  42.8 1.0 %collective-permute-done.6.refs_0_ = bf16[2,8,80,128]{3,2,1,0:T(8,128)(2,1)S(1)} collective-permute-done((bf16[2,8,80,128]{3,2,1,0:T(8,128)(2,1)S(1)}, bf16[2,8,80,128]{3,2,1,0:T(8,128)(2,1)S(1)}, u32[]{:S(2)}, u32[]{:S(2)}) %collective-permute-start.6) | collective-permute-done | bytes 327712 | tf_op jit(solution)/shard_map/ppermute | solution.py:586
  43.8 3.2 %shard_map.170 = (f32[2,32,224,128]{3,2,1,0:T(8,128)S(1)}, f32[240,256]{1,0:T(8,128)S(1)}, f32[256,256]{1,0:T(8,128)S(1)}, f32[80,256]{1,0:T(8,128)S(1)}, f32[22...) custom-call(bf16[2,8,80,128]{3,2,1,0:T(8,128)(2,1)S(1)} %get-tuple-element.116.own_ref, ...), custom_call_target="tpu_custom_call", output_to_operand_aliasing={{0}: (17, {})} | custom-call | tf_op jit(solution)/shard_map/pallas_call | solution.py:562
  47.0 0.3 collective-permute-done.5.refs_0_
  47.3 1.4 %shard_map.171 = (f32[2,32,224,128]{3,2,1,0:T(8,128)S(1)}, f32[240,256]{1,0:T(8,128)S(1)}, f32[256,256]{1,0:T(8,128)S(1)}, f32[80,256]{1,0:T(8,128)S(1)}, f32[22...) custom-call(bf16[2,4,80,128]{3,2,1,0:T(8,128)(2,1)S(1)} %get-tuple-element.109.own_ref, ...), custom_call_target="tpu_custom_call", output_to_operand_aliasing={{0}: (17, {})} | custom-call | tf_op jit(solution)/shard_map/pallas_call | solution.py:562
  48.7 2.1 %collective-permute-done.2.refs_0_ = bf16[2,4,80,128]{3,2,1,0:T(8,128)(2,1)S(1)} collective-permute-done((bf16[2,4,80,128]{3,2,1,0:T(8,128)(2,1)S(1)}, bf16[2,4,80,128]{3,2,1,0:T(8,128)(2,1)S(1)}, u32[]{:S(2)}, u32[]{:S(2)}) %collective-permute-start.2) | collective-permute-done | bytes 163872 | tf_op jit(solution)/shard_map/ppermute | solution.py:586
  50.8 2.3 %shard_map.172 = (f32[2,32,224,128]{3,2,1,0:T(8,128)S(1)}, f32[240,256]{1,0:T(8,128)}, f32[256,256]{1,0:T(8,128)}, f32[80,256]{1,0:T(8,128)}, f32[224,128]{1,0:T...) custom-call(bf16[2,4,80,128]{3,2,1,0:T(8,128)(2,1)S(1)} %get-tuple-e, ...), custom_call_target="tpu_custom_call", output_to_operand_aliasing={{0}: (17, {})} | custom-call | tf_op jit(solution)/shard_map/pallas_call | solution.py:562
  53.1 0.8 collective-permute-start.13
  53.9 1.0 %collective-permute-done.13.refs_1_ = bf16[320,256]{1,0:T(8,128)(2,1)S(1)} collective-permute-done((bf16[320,256]{1,0:T(8,128)(2,1)S(1)}, bf16[320,256]{1,0:T(8,128)(2,1)S(1)}, u32[]{:S(2)}, u32[]{:S(2)}) %collective-permute-start.13) | collective-permute-done | bytes 163872 | tf_op jit(solution)/shard_map/ppermute | solution.py:399
  55.0 0.6 collective-permute-start.14
  55.6 4.2 %collective-permute-done.14.refs_1_ = bf16[160,256]{1,0:T(8,128)(2,1)S(1)} collective-permute-done((bf16[160,256]{1,0:T(8,128)(2,1)S(1)}, bf16[160,256]{1,0:T(8,128)(2,1)S(1)}, u32[]{:S(2)}, u32[]{:S(2)}) %collective-permute-start.14) | collective-permute-done | bytes 81952 | tf_op jit(solution)/shard_map/ppermute | solution.py:399
  59.8 1.6 %collective-permute-start.15 = (bf16[160,256]{1,0:T(8,128)(2,1)S(1)}, bf16[160,256]{1,0:T(8,128)(2,1)S(1)}, u32[]{:S(2)}, u32[]{:S(2)}) collective-permute-start(bf16[160,256]{1,0:T(8,128)(2,1)S(1)} %add_parts.5.refs_0_), channel_id=1, source_target_pairs={{0,16},{16,0},{1,17},{17,1},{2,18},{18,2},{3,19},{19,3},{4,20},{20... | collective-permute-start | bytes 245768 | tf_op jit(solution)/shard_map/ppermute | solution.py:403
  61.4 3.0 %collective-permute-done.15.refs_1_ = bf16[160,256]{1,0:T(8,128)(2,1)S(1)} collective-permute-done((bf16[160,256]{1,0:T(8,128)(2,1)S(1)}, bf16[160,256]{1,0:T(8,128)(2,1)S(1)}, u32[]{:S(2)}, u32[]{:S(2)}) %collective-permute-start.15) | collective-permute-done | bytes 81952 | tf_op jit(solution)/shard_map/ppermute | solution.py:403
  64.4 1.0 %collective-permute-start.16 = (bf16[160,256]{1,0:T(8,128)(2,1)S(1)}, bf16[160,256]{1,0:T(8,128)(2,1)S(1)}, u32[]{:S(2)}, u32[]{:S(2)}) collective-permute-start(bf16[160,256]{1,0:T(8,128)(2,1)S(1)} %add_parts.6.refs_0_), channel_id=1, source_target_pairs={{0,1},{1,2},{2,3},{3,0},{4,5},{5,6},{6,7},{7,4},{8,9},{9,10},{10,1... | collective-permute-start | bytes 245768 | tf_op jit(solution)/shard_map/ppermute | solution.py:403
  65.4 3.5 %collective-permute-start.17 = (bf16[160,256]{1,0:T(8,128)(2,1)S(1)}, bf16[160,256]{1,0:T(8,128)(2,1)S(1)}, u32[]{:S(2)}, u32[]{:S(2)}) collective-permute-start(bf16[160,256]{1,0:T(8,128)(2,1)S(1)} %add_parts.6.refs_0_), channel_id=1, source_target_pairs={{0,2},{1,3},{2,0},{3,1},{4,6},{5,7},{6,4},{7,5},{8,10},{9,11},{10,... | collective-permute-start | bytes 245768 | tf_op jit(solution)/shard_map/ppermute | solution.py:403
  68.9 1.2 %collective-permute-start.18 = (bf16[160,256]{1,0:T(8,128)(2,1)S(1)}, bf16[160,256]{1,0:T(8,128)(2,1)S(1)}, u32[]{:S(2)}, u32[]{:S(2)}) collective-permute-start(bf16[160,256]{1,0:T(8,128)(2,1)S(1)} %add_parts.6.refs_0_), channel_id=1, source_target_pairs={{0,3},{1,0},{2,1},{3,2},{4,7},{5,4},{6,5},{7,6},{8,11},{9,8},{10,9... | collective-permute-start | bytes 245768 | tf_op jit(solution)/shard_map/ppermute | solution.py:403
  70.0 1.2 %collective-permute-done.16.refs_1_ = bf16[160,256]{1,0:T(8,128)(2,1)S(1)} collective-permute-done((bf16[160,256]{1,0:T(8,128)(2,1)S(1)}, bf16[160,256]{1,0:T(8,128)(2,1)S(1)}, u32[]{:S(2)}, u32[]{:S(2)}) %collective-permute-start.16) | collective-permute-done | bytes 81952 | tf_op jit(solution)/shard_map/ppermute | solution.py:403
  71.2 2.3 %collective-permute-done.17.refs_2_ = bf16[160,256]{1,0:T(8,128)(2,1)S(1)} collective-permute-done((bf16[160,256]{1,0:T(8,128)(2,1)S(1)}, bf16[160,256]{1,0:T(8,128)(2,1)S(1)}, u32[]{:S(2)}, u32[]{:S(2)}) %collective-permute-start.17) | collective-permute-done | bytes 81952 | tf_op jit(solution)/shard_map/ppermute | solution.py:403
  73.5 0.4 collective-permute-done.18.refs_3_
  74.0 0.5 collective-permute-start.19
  74.4 4.0 %collective-permute-done.19.other_ref = bf16[160,256]{1,0:T(8,128)(2,1)S(1)} collective-permute-done((bf16[160,256]{1,0:T(8,128)(2,1)S(1)}, bf16[160,256]{1,0:T(8,128)(2,1)S(1)}, u32[]{:S(2)}, u32[]{:S(2)}) %collective-permute-start.19) | collective-permute-done | bytes 81952 | tf_op jit(solution)/shard_map/ppermute | solution.py:399
  78.6 0.7 collective-permute-start.10
  79.3 1.8 %collective-permute-start.9 = (bf16[2,224,128]{2,1,0:T(8,128)(2,1)S(1)}, bf16[2,224,128]{2,1,0:T(8,128)(2,1)S(1)}, u32[]{:S(2)}, u32[]{:S(2)}) collective-permute-start(bf16[2,224,128]{2,1,0:T(8,128)(2,1)S(1)} %get-tuple-element.162), channel_id=1, source_target_pairs={{0,4},{8,12},{4,0},{12,8},{1,5},{9,13},{5,1},{13,9},{2,6},{10,14},... | collective-permute-start | bytes 344072 | tf_op jit(solution)/shard_map/ppermute | solution.py:395
  81.1 1.2 %collective-permute-start.11 = (bf16[224,128]{1,0:T(8,128)(2,1)S(1)}, bf16[224,128]{1,0:T(8,128)(2,1)S(1)}, u32[]{:S(2)}, u32[]{:S(2)}) collective-permute-start(bf16[224,128]{1,0:T(8,128)(2,1)S(1)} %get-tuple-element.164), channel_id=1, source_target_pairs={{0,1},{1,2},{2,3},{3,0},{4,5},{5,6},{6,7},{7,4},{8,9},{9,10},{10,1... | collective-permute-start | bytes 172040 | tf_op jit(solution)/shard_map/ppermute | solution.py:595
  82.3 2.6 %collective-permute-start.12 = (bf16[224,128]{1,0:T(8,128)(2,1)S(1)}, bf16[224,128]{1,0:T(8,128)(2,1)S(1)}, u32[]{:S(2)}, u32[]{:S(2)}) collective-permute-start(bf16[224,128]{1,0:T(8,128)(2,1)S(1)} %get-tuple-element.164), channel_id=1, source_target_pairs={{0,3},{1,0},{2,1},{3,2},{4,7},{5,4},{6,5},{7,6},{8,11},{9,8},{10,9... | collective-permute-start | bytes 172040 | tf_op jit(solution)/shard_map/ppermute | solution.py:596
  84.9 2.5 %collective-permute-done.11.left_ref = bf16[224,128]{1,0:T(8,128)(2,1)S(1)} collective-permute-done((bf16[224,128]{1,0:T(8,128)(2,1)S(1)}, bf16[224,128]{1,0:T(8,128)(2,1)S(1)}, u32[]{:S(2)}, u32[]{:S(2)}) %collective-permute-start.11) | collective-permute-done | bytes 57376 | tf_op jit(solution)/shard_map/ppermute | solution.py:595
  87.5 3.4 %final.2.refs_0_ = bf16[2,222,32,128]{3,2,1,0:T(8,128)(2,1)} custom-call(f32[2,32,224,128]{3,2,1,0:T(8,128)S(1)} %get-tuple-element.161.g_ref, bf16[2,224,128]{2,1,0:T(8,128)(2,1)S(1)} %collective-permute-done.9.first_ref, bf16[2,224,128]{2,1,0:T(8,128)(2,1)S(1)} %collective-permute-done.10.second_ref, ...), custom_call_target="tpu_custom_call" | custom-call | tf_op jit(solution)/shard_map/final/pallas_call | solution.py:602
  90.9 3.4 %final.3 = bf16[2,222,32,128]{3,2,1,0:T(8,128)(2,1)} custom-call(f32[2,32,224,128]{3,2,1,0:T(8,128)S(1)} %get-tuple-element.161.g_ref, bf16[2,224,128]{2,1,0:T(8,128)(2,1)S(1)} %collective-permute-done.9.first_ref, bf16[2,224,128]{2,1,0:T(8,128)(2,1)S(1)} %collective-permute-done.10.second_ref, ...), custom_call_target="tpu_custom_call", output_to_operand_aliasing={{}: (6, {})} | custom-call | tf_op jit(solution)/shard_map/final/pallas_call | solution.py:602
  94.3 1.0 %unpack.1 = (f32[222,256]{1,0:T(8,128)}, f32[16,256]{1,0:T(8,128)}, f32[256,256]{1,0:T(8,128)}, f32[222,256]{1,0:T(8,128)}, f32[1,222]{1,0:T(1,128)}) custom-call(bf16[320,256]{1,0:T(8,128)(2,1)S(1)} %join_halves.1.mine_ref, bf16[320,256]{1,0:T(8,128)(2,1)S(1)} %collective-permute-done.20.other_ref, bf16[240,222]{1,0:T(8,128)(2,1)S(1)} %copy-done.1, ...), custom_call_target="tpu_custom_call" | custom-call | tf_op jit(solution)/shard_map/unpack/pallas_call | solution.py:638
  (20 shorter events, 0.3 us)
Async XLA Ops:
  7.8 17.9 %collective-permute-start.3 = (bf16[2,224,128]{2,1,0:T(8,128)(2,1)S(1)}, bf16[2,224,128]{2,1,0:T(8,128)(2,1)S(1)}, u32[]{:S(2)}, u32[]{:S(2)}) collective-permute-start(bf16[2,224,128]{2,1,0:T(8,128)(2,1)S(1)} %get-tuple-element.107), channel_id=1, source_target_pairs={{0,4},{8,12},{4,0},{12,8},{1,5},{9,13},{5,1},{13,9},{2,6},{10,14},... | collective-permute-start | bytes 344072 | tf_op jit(solution)/shard_map/ppermute | solution.py:395
  8.4 17.3 %collective-permute-start.4 = (bf16[2,224,128]{2,1,0:T(8,128)(2,1)S(1)}, bf16[2,224,128]{2,1,0:T(8,128)(2,1)S(1)}, u32[]{:S(2)}, u32[]{:S(2)}) collective-permute-start(bf16[2,224,128]{2,1,0:T(8,128)(2,1)S(1)} %get-tuple-element.108), channel_id=1, source_target_pairs={{4,8},{8,4},{5,9},{9,5},{6,10},{10,6},{7,11},{11,7},{20,24},{24,20... | collective-permute-start | bytes 344072 | tf_op jit(solution)/shard_map/ppermute | solution.py:395
  9.0 6.9 %collective-permute-start = (bf16[224,128]{1,0:T(8,128)(2,1)S(1)}, bf16[224,128]{1,0:T(8,128)(2,1)S(1)}, u32[]{:S(2)}, u32[]{:S(2)}) collective-permute-start(bf16[224,128]{1,0:T(8,128)(2,1)S(1)} %get-tuple-element.91), channel_id=1, source_target_pairs={{0,1},{1,2},{2,3},{3,0},{4,5},{5,6},{6,7},{7,4},{8,9},{9,10},{10,1... | collective-permute-start | bytes 172040 | tf_op jit(solution)/shard_map/ppermute | solution.py:495
  11.7 4.8 %collective-permute-start.1 = (bf16[224,128]{1,0:T(8,128)(2,1)S(1)}, bf16[224,128]{1,0:T(8,128)(2,1)S(1)}, u32[]{:S(2)}, u32[]{:S(2)}) collective-permute-start(bf16[224,128]{1,0:T(8,128)(2,1)S(1)} %get-tuple-element.91), channel_id=1, source_target_pairs={{0,3},{1,0},{2,1},{3,2},{4,7},{5,4},{6,5},{7,6},{8,11},{9,8},{10,9... | collective-permute-start | bytes 172040 | tf_op jit(solution)/shard_map/ppermute | solution.py:495
  20.1 16.7 %collective-permute-start.8 = (bf16[2,8,80,128]{3,2,1,0:T(8,128)(2,1)S(1)}, bf16[2,8,80,128]{3,2,1,0:T(8,128)(2,1)S(1)}, u32[]{:S(2)}, u32[]{:S(2)}) collective-permute-start(bf16[2,8,80,128]{3,2,1,0:T(8,128)(2,1)S(1)} %get-tuple-element.130.own_ref), channel_id=1, source_target_pairs={{0,16},{16,0},{1,17},{17,1},{2,18},{18,2},{3,19},{19,3},{4,20},{20... | collective-permute-start | bytes 983048 | tf_op jit(solution)/shard_map/ppermute | solution.py:586
  25.1 14.7 %collective-permute-start.7 = (bf16[2,8,80,128]{3,2,1,0:T(8,128)(2,1)S(1)}, bf16[2,8,80,128]{3,2,1,0:T(8,128)(2,1)S(1)}, u32[]{:S(2)}, u32[]{:S(2)}) collective-permute-start(bf16[2,8,80,128]{3,2,1,0:T(8,128)(2,1)S(1)} %get-tuple-element.123.own_ref), channel_id=1, source_target_pairs={{0,16},{16,0},{1,17},{17,1},{2,18},{18,2},{3,19},{19,3},{4,20},{20... | collective-permute-start | bytes 983048 | tf_op jit(solution)/shard_map/ppermute | solution.py:586
  29.2 7.2 %copy-start = (f32[6,13,32,128]{3,2,1,0:T(8,128)S(1)}, f32[6,13,32,128]{3,2,1,0:T(8,128)}, u32[]{:S(2)}) copy-start(f32[6,13,32,128]{3,2,1,0:T(8,128)} %param.14) | copy-start | bytes 3833860
  29.2 14.6 %collective-permute-start.6 = (bf16[2,8,80,128]{3,2,1,0:T(8,128)(2,1)S(1)}, bf16[2,8,80,128]{3,2,1,0:T(8,128)(2,1)S(1)}, u32[]{:S(2)}, u32[]{:S(2)}) collective-permute-start(bf16[2,8,80,128]{3,2,1,0:T(8,128)(2,1)S(1)} %get-tuple-element.116.own_ref), channel_id=1, source_target_pairs={{0,16},{16,0},{1,17},{17,1},{2,18},{18,2},{3,19},{19,3},{4,20},{20... | collective-permute-start | bytes 983048 | tf_op jit(solution)/shard_map/ppermute | solution.py:586
  32.5 14.8 %collective-permute-start.5 = (bf16[2,4,80,128]{3,2,1,0:T(8,128)(2,1)S(1)}, bf16[2,4,80,128]{3,2,1,0:T(8,128)(2,1)S(1)}, u32[]{:S(2)}, u32[]{:S(2)}) collective-permute-start(bf16[2,4,80,128]{3,2,1,0:T(8,128)(2,1)S(1)} %get-tuple-element.109.own_ref), channel_id=1, source_target_pairs={{0,16},{16,0},{1,17},{17,1},{2,18},{18,2},{3,19},{19,3},{4,20},{20... | collective-permute-start | bytes 491528 | tf_op jit(solution)/shard_map/ppermute | solution.py:586
  34.8 16.0 %collective-permute-start.2 = (bf16[2,4,80,128]{3,2,1,0:T(8,128)(2,1)S(1)}, bf16[2,4,80,128]{3,2,1,0:T(8,128)(2,1)S(1)}, u32[]{:S(2)}, u32[]{:S(2)}) collective-permute-start(bf16[2,4,80,128]{3,2,1,0:T(8,128)(2,1)S(1)} %get-tuple-element.98.own_ref), channel_id=1, source_target_pairs={{0,16},{16,0},{1,17},{17,1},{2,18},{18,2},{3,19},{19,3},{4,20},{20... | collective-permute-start | bytes 491528 | tf_op jit(solution)/shard_map/ppermute | solution.py:586
  53.1 1.8 %collective-permute-start.13 = (bf16[320,256]{1,0:T(8,128)(2,1)S(1)}, bf16[320,256]{1,0:T(8,128)(2,1)S(1)}, u32[]{:S(2)}, u32[]{:S(2)}) collective-permute-start(bf16[320,256]{1,0:T(8,128)(2,1)S(1)} %get-tuple-element.166), channel_id=1, source_target_pairs={{0,4},{4,0},{8,12},{12,8},{1,5},{5,1},{9,13},{13,9},{2,6},{6,2},{1... | collective-permute-start | bytes 491528 | tf_op jit(solution)/shard_map/ppermute | solution.py:399
  55.0 4.8 %collective-permute-start.14 = (bf16[160,256]{1,0:T(8,128)(2,1)S(1)}, bf16[160,256]{1,0:T(8,128)(2,1)S(1)}, u32[]{:S(2)}, u32[]{:S(2)}) collective-permute-start(bf16[160,256]{1,0:T(8,128)(2,1)S(1)} %get-tuple-element.168), channel_id=1, source_target_pairs={{0,8},{4,12},{8,0},{12,4},{1,9},{5,13},{9,1},{13,5},{2,10},{6,14},... | collective-permute-start | bytes 245768 | tf_op jit(solution)/shard_map/ppermute | solution.py:399
  59.8 4.5 %collective-permute-start.15 = (bf16[160,256]{1,0:T(8,128)(2,1)S(1)}, bf16[160,256]{1,0:T(8,128)(2,1)S(1)}, u32[]{:S(2)}, u32[]{:S(2)}) collective-permute-start(bf16[160,256]{1,0:T(8,128)(2,1)S(1)} %add_parts.5.refs_0_), channel_id=1, source_target_pairs={{0,16},{16,0},{1,17},{17,1},{2,18},{18,2},{3,19},{19,3},{4,20},{20... | collective-permute-start | bytes 245768 | tf_op jit(solution)/shard_map/ppermute | solution.py:403
  64.4 6.8 %collective-permute-start.16 = (bf16[160,256]{1,0:T(8,128)(2,1)S(1)}, bf16[160,256]{1,0:T(8,128)(2,1)S(1)}, u32[]{:S(2)}, u32[]{:S(2)}) collective-permute-start(bf16[160,256]{1,0:T(8,128)(2,1)S(1)} %add_parts.6.refs_0_), channel_id=1, source_target_pairs={{0,1},{1,2},{2,3},{3,0},{4,5},{5,6},{6,7},{7,4},{8,9},{9,10},{10,1... | collective-permute-start | bytes 245768 | tf_op jit(solution)/shard_map/ppermute | solution.py:403
  65.4 8.2 %collective-permute-start.17 = (bf16[160,256]{1,0:T(8,128)(2,1)S(1)}, bf16[160,256]{1,0:T(8,128)(2,1)S(1)}, u32[]{:S(2)}, u32[]{:S(2)}) collective-permute-start(bf16[160,256]{1,0:T(8,128)(2,1)S(1)} %add_parts.6.refs_0_), channel_id=1, source_target_pairs={{0,2},{1,3},{2,0},{3,1},{4,6},{5,7},{6,4},{7,5},{8,10},{9,11},{10,... | collective-permute-start | bytes 245768 | tf_op jit(solution)/shard_map/ppermute | solution.py:403
  68.9 5.0 %collective-permute-start.18 = (bf16[160,256]{1,0:T(8,128)(2,1)S(1)}, bf16[160,256]{1,0:T(8,128)(2,1)S(1)}, u32[]{:S(2)}, u32[]{:S(2)}) collective-permute-start(bf16[160,256]{1,0:T(8,128)(2,1)S(1)} %add_parts.6.refs_0_), channel_id=1, source_target_pairs={{0,3},{1,0},{2,1},{3,2},{4,7},{5,4},{6,5},{7,6},{8,11},{9,8},{10,9... | collective-permute-start | bytes 245768 | tf_op jit(solution)/shard_map/ppermute | solution.py:403
  74.0 4.5 %collective-permute-start.19 = (bf16[160,256]{1,0:T(8,128)(2,1)S(1)}, bf16[160,256]{1,0:T(8,128)(2,1)S(1)}, u32[]{:S(2)}, u32[]{:S(2)}) collective-permute-start(bf16[160,256]{1,0:T(8,128)(2,1)S(1)} %add_parts.7.mine_ref), channel_id=1, source_target_pairs={{0,8},{4,12},{8,0},{12,4},{1,9},{5,13},{9,1},{13,5},{2,10},{6,14},... | collective-permute-start | bytes 245768 | tf_op jit(solution)/shard_map/ppermute | solution.py:399
  78.5 15.8 %collective-permute-start.20 = (bf16[320,256]{1,0:T(8,128)(2,1)S(1)}, bf16[320,256]{1,0:T(8,128)(2,1)S(1)}, u32[]{:S(2)}, u32[]{:S(2)}) collective-permute-start(bf16[320,256]{1,0:T(8,128)(2,1)S(1)} %join_halves.1.mine_ref), channel_id=1, source_target_pairs={{0,4},{4,0},{8,12},{12,8},{1,5},{5,1},{9,13},{13,9},{2,6},{6,2},{1... | collective-permute-start | bytes 491528 | tf_op jit(solution)/shard_map/ppermute | solution.py:399
  78.6 8.9 %collective-permute-start.10 = (bf16[2,224,128]{2,1,0:T(8,128)(2,1)S(1)}, bf16[2,224,128]{2,1,0:T(8,128)(2,1)S(1)}, u32[]{:S(2)}, u32[]{:S(2)}) collective-permute-start(bf16[2,224,128]{2,1,0:T(8,128)(2,1)S(1)} %get-tuple-element.163), channel_id=1, source_target_pairs={{4,8},{8,4},{5,9},{9,5},{6,10},{10,6},{7,11},{11,7},{20,24},{24,20... | collective-permute-start | bytes 344072 | tf_op jit(solution)/shard_map/ppermute | solution.py:395
  79.3 8.2 %collective-permute-start.9 = (bf16[2,224,128]{2,1,0:T(8,128)(2,1)S(1)}, bf16[2,224,128]{2,1,0:T(8,128)(2,1)S(1)}, u32[]{:S(2)}, u32[]{:S(2)}) collective-permute-start(bf16[2,224,128]{2,1,0:T(8,128)(2,1)S(1)} %get-tuple-element.162), channel_id=1, source_target_pairs={{0,4},{8,12},{4,0},{12,8},{1,5},{9,13},{5,1},{13,9},{2,6},{10,14},... | collective-permute-start | bytes 344072 | tf_op jit(solution)/shard_map/ppermute | solution.py:395
  81.1 6.4 %collective-permute-start.11 = (bf16[224,128]{1,0:T(8,128)(2,1)S(1)}, bf16[224,128]{1,0:T(8,128)(2,1)S(1)}, u32[]{:S(2)}, u32[]{:S(2)}) collective-permute-start(bf16[224,128]{1,0:T(8,128)(2,1)S(1)} %get-tuple-element.164), channel_id=1, source_target_pairs={{0,1},{1,2},{2,3},{3,0},{4,5},{5,6},{6,7},{7,4},{8,9},{9,10},{10,1... | collective-permute-start | bytes 172040 | tf_op jit(solution)/shard_map/ppermute | solution.py:595
  82.3 5.2 %collective-permute-start.12 = (bf16[224,128]{1,0:T(8,128)(2,1)S(1)}, bf16[224,128]{1,0:T(8,128)(2,1)S(1)}, u32[]{:S(2)}, u32[]{:S(2)}) collective-permute-start(bf16[224,128]{1,0:T(8,128)(2,1)S(1)} %get-tuple-element.164), channel_id=1, source_target_pairs={{0,3},{1,0},{2,1},{3,2},{4,7},{5,4},{6,5},{7,6},{8,11},{9,8},{10,9... | collective-permute-start | bytes 172040 | tf_op jit(solution)/shard_map/ppermute | solution.py:596
  90.9 3.4 %copy-start.1 = (bf16[240,222]{1,0:T(8,128)(2,1)S(1)}, bf16[240,222]{1,0:T(8,128)(2,1)}, u32[]{:S(2)}) copy-start(bf16[240,222]{1,0:T(8,128)(2,1)} %constant.8.clone.refs_5_.place_ref) | copy-start | bytes 319684
  90.9 3.4 %copy-start.2 = (bf16[222,80]{1,0:T(8,128)(2,1)S(1)}, bf16[222,80]{1,0:T(8,128)(2,1)}, u32[]{:S(2)}) copy-start(bf16[222,80]{1,0:T(8,128)(2,1)} %constant.10.clone.refs_7_.scat_ref) | copy-start | bytes 106564
